TPU v7x, 32 devices: a whole 2x2x4 slice. The times are simulated.
32 devices in a mesh: parts: 2 (over y), tm: 16 (over z, x, core).
Axes of the slice: x: 2, y: 2, z: 4, core: 2. Of those that a mesh axis runs over, the one named last changes fastest.
Arguments:
- signal: bfloat16 [16384, 1024], P(('parts', 'tm')), parts along dimension 0, may hold values from -6 to 6
- pool_weight: bfloat16 [4096, 2048], P('tm'), may hold values from -0.09375 to 0.09375
- norm_gain: float32 [2, 2048], replicated, may hold values from 0.1 to 1.9
- step_size: float32 [2, 2048], replicated, may hold values from 0 to 0.05, as said below
- mode_out: float32 [2, 32, 2048], replicated, may hold values from -1 to 1
- skip_gain: float32 [2, 2048], replicated, may hold values from -4 to 4
Outputs:
- pooled_out: bfloat16 [4096, 2048], P(('parts', 'tm')), parts along dimension 0
There are 2 independent parts, one for each index of `parts`. A program takes and returns all parts, laid end to end along the dimension named above; an argument that names none is the same for every part. Nothing has to cross between parts.
Inputs may be any that keep to these rules, and one draw needn't show every extreme that they name: `step_size`: positive step sizes.
All inputs are finite; a program needn't handle non-finite values.
Results may differ from a plain program's by a relative error of at most 0.001.
Values may be sent and summed in bfloat16 or wider, within the bound.
A program may use at most 320 MiB of HBM per device.

v0:
```python
import jax
import jax.numpy as jnp
from jax import lax
from jax.sharding import PartitionSpec as P

POOL = 4


def prefix_2(value, axis, join, neutral):
    count, mine = (lax.axis_size(axis), lax.axis_index(axis))
    pieces = jax.tree.map(lambda part: lax.all_gather(part, axis), value)
    running = jax.tree.map(
        lambda part, zero: jnp.full_like(part, 0) + jnp.asarray(zero, part.dtype), value, neutral
    )

    def turn(position, running):
        longer = join(running, jax.tree.map(lambda part: part[position], pieces))
        return jax.tree.map(lambda new, old: jnp.where(position < mine, new, old), longer, running)

    return lax.fori_loop(0, count - 1, turn, running)


def build_tables(decay_rates, in_scale, out_mix, block_len):
    lag_steps = jnp.arange(block_len, dtype=jnp.float32)
    powers = jnp.exp(-lag_steps[:, None, None] * decay_rates[None])
    kernel = jnp.sum(out_mix[None] * in_scale[None] * powers, axis=1)
    lag_index = jnp.arange(block_len, dtype=jnp.int32)
    lag_gap = lag_index[:, None] - lag_index[None, :]
    picked = kernel[jnp.clip(lag_gap, 0, block_len - 1)]
    toeplitz = jnp.where((lag_gap >= 0)[:, :, None], picked, jnp.zeros_like(picked))
    into_table = in_scale[None] * jnp.exp(
        -(block_len - 1 - lag_steps)[:, None, None] * decay_rates[None]
    )
    outof_table = out_mix[None] * jnp.exp(-(lag_steps + 1.0)[:, None, None] * decay_rates[None])
    return (toeplitz, into_table, outof_table)


def layer_norm(hidden, gain_row):
    row_mean = jnp.mean(hidden, axis=-1, keepdims=True)
    centered = hidden - row_mean
    row_var = jnp.mean(centered * centered, axis=-1, keepdims=True)
    return centered * lax.rsqrt(row_var + 1e-05) * gain_row[None, :]


def earlier_states(device_end, decay_rates, row_count):

    def combine(earlier, later_pair):
        return (earlier[0] * later_pair[0], later_pair[0] * earlier[1] + later_pair[1])

    device_decay = jnp.exp(-decay_rates * row_count)
    prefix = prefix_2(
        (device_decay, device_end),
        "tm",
        combine,
        (jnp.ones_like(device_decay), jnp.zeros_like(device_end)),
    )
    return prefix[1]


def state_layer(hidden, gain_row, step_row, out_mix, skip_row):
    row_count, chan_count = hidden.shape
    modes = out_mix.shape[0]
    block_len = min(16, row_count)
    blocks = row_count // block_len
    normed = layer_norm(hidden, gain_row)
    decay_rates = step_row[None, :] * (jnp.arange(modes, dtype=jnp.float32) + 1.0)[:, None]
    in_scale = jnp.sqrt(-jnp.expm1(-2.0 * decay_rates))
    toeplitz, into_table, outof_table = build_tables(decay_rates, in_scale, out_mix, block_len)
    block_decay = jnp.exp(-decay_rates * block_len)
    exact = lax.Precision.HIGHEST
    grouped = normed.reshape(blocks, block_len, chan_count)
    block_ends = jnp.einsum("snh,bsh->bnh", into_table, grouped, precision=exact)

    def advance(state, block_end):
        return (block_decay * state + block_end, state)

    start_state = jnp.zeros((modes, chan_count), jnp.float32)
    device_end, local_in = lax.scan(advance, start_state, block_ends)
    incoming = earlier_states(device_end, decay_rates, row_count)
    inner = jnp.einsum("tsh,bsh->bth", toeplitz, grouped, precision=exact)
    offsets = jnp.arange(blocks, dtype=jnp.float32) * block_len
    full_in = local_in + jnp.exp(-decay_rates[None] * offsets[:, None, None]) * incoming[None]
    carried = jnp.einsum("tnh,bnh->bth", outof_table, full_in, precision=exact)
    response = inner + carried + skip_row[None, None, :] * grouped
    return hidden + jax.nn.gelu(response, approximate=False).reshape(row_count, chan_count)


def local(signal, pool_weight, norm_gain, step_size, mode_out, skip_gain):
    fine_rows, channels = signal.shape
    row_count = fine_rows // POOL
    coarse = signal.reshape(row_count, POOL * channels)
    full_weight = lax.all_gather(pool_weight, "tm", axis=0, tiled=True)
    hidden = jnp.dot(coarse, full_weight, preferred_element_type=jnp.float32)
    for layer_index in range(norm_gain.shape[0]):
        hidden = state_layer(
            hidden,
            norm_gain[layer_index],
            step_size[layer_index],
            mode_out[layer_index],
            skip_gain[layer_index],
        )
    return hidden.astype(jnp.bfloat16)


def solution(mesh):
    placed = (P(("parts", "tm"), None), P("tm", None), P(), P(), P(), P())
    return jax.shard_map(
        local, mesh=mesh, in_specs=placed, out_specs=P(("parts", "tm"), None), check_vma=False
    )
```

profile of v0, /device:TPU:0, one launch (start us, length us, event | category | flops | bytes accessed | tf_op | source)
XLA Modules:
  0.0 565.8 jit_solution(8745183062602447710)
XLA Ops:
  8.1 2.4 slice_bitcast_fusion
  12.1 1.3 copy.80
  13.4 1.4 reshape.456
  15.5 123.2 %all-gather.8.cloned.1.call-done = bf16[4096,2048]{1,0:T(8,128)(2,1)} async-done(((bf16[256,2048]{1,0:T(8,128)(2,1)}), bf16[4096,2048]{1,0:T(8,128)(2,1)}) %all-gather.8.cloned.1.call-update) | async-done | bytes 16777232 | tf_op jit(solution)/shard_map/all_gather | solution.py:92
  138.7 8.5 %fusion.87 = (f32[128]{0:T(128)S(1)}, f32[128,2048]{1,0:T(8,128)S(1)}) fusion(bf16[128,4096]{1,0:T(8,128)(2,1)} %reshape.456, bf16[4096,2048]{1,0:T(8,128)(2,1)} %all-gather.8.cloned.1.call-done), kind=kOutput, calls=%fused_computation.147 | convolution fusion | flops 2147745792 | bytes 18874880 | tf_op jit(solution)/shard_map/dot_general | solution.py:93
  148.7 6.0 %copy.79 = f32[8,16,2048]{1,0,2:T(8,128)} copy(f32[8,16,2048]{2,1,0:T(8,128)} %bitcast.89) | data formatting | bytes 2097152 | tf_op jit(solution)/shard_map/reshape | solution.py:71
  154.7 22.8 %fusion.42 = f32[8,32,2048]{1,0,2:T(8,128)} fusion(f32[8,16,2048]{1,0,2:T(8,128)} %copy.79, f32[16]{0:T(128)S(1)} %subtract_negate_fusion, f32[32,2048]{0,1:T(8,128)} %copy.80, f32[32,2048]{0,1:T(8,128)S(1)} %copy.76), kind=kOutput, calls=%fused_computation.54 | convolution fusion | flops 102760448 | bytes 3670080 | tf_op jit(solution)/shard_map/snh,bsh->bnh/dot_general | solution.py:72
  177.5 6.3 %copy.82 = f32[8,32,2048]{2,1,0:T(8,128)} copy(f32[8,32,2048]{1,0,2:T(8,128)} %fusion.42) | data formatting | bytes 4194304
  183.8 1.6 broadcast.473.clone
  185.4 14.7 %while.54 = (s32[]{:T(128)}, f32[32,2048]{1,0:T(8,128)S(1)}, f32[8,32,2048]{2,1,0:T(8,128)}, f32[8,32,2048]{2,1,0:T(8,128)}, f32[32]{0:T(128)S(1)}, /*index=5*/f32[2048]{0:T(1024)S(1)}, s32[]{:T(128)}, s32[]{:T(128)}) while((s32[]{:T(128)}, f32[32,2048]{1,0:T(8,128)S(1)}, f32[8,32,2048]{2,1,0:T(8,128)}, f32[8,32,2048]{2,1,0:T(8,128)}, ...), condition=%wide.region_4.5_spmd.clone, body=%wide.region_3.4_spmd.clone.sunk | while | flops 458755 | bytes 1319652 | solution.py:78
  203.8 1.3 copy.83
  205.1 1.3 copy.88
  206.4 2.4 copy.75
  208.8 2.3 copy.87
  211.1 26.7 %multiply_reduce_fusion = (f32[16,2048]{0,1:T(8,128)}, f32[16,2048]{0,1:T(8,128)}) fusion(f32[32,2048]{0,1:T(8,128)S(1)} %copy.88, f32[32,2048]{0,1:T(8,128)} %copy.87, f32[16]{0:T(128)S(1)} %iota_negate_fusion, f32[32,2048]{0,1:T(8,128)S(1)} %copy.76, f32[32,2048]{0,1:T(8,128)} %copy.75), kind=kLoop, calls=%fused_computation.26 | loop fusion | flops 6225920 | bytes 1310784 | tf_op jit(solution)/shard_map/reduce_sum | solution.py:26
  237.8 1.5 copy.77
  239.3 1.3 reshape.463
  241.3 2.8 gather_fusion
  244.0 12.0 %copy.78 = f32[16,16,2048]{1,0,2:T(8,128)} copy(f32[16,16,2048]{2,1,0:T(8,128)} %bitcast.94) | data formatting | bytes 4194304 | tf_op jit(solution)/shard_map/gather | solution.py:29
  256.6 2.3 copy.92
  258.9 31.3 %fusion.24 = f32[2048,8,16]{2,1,0:T(8,128)} fusion(f32[8,16,2048]{1,0,2:T(8,128)} %copy.79, f32[16,16,2048]{1,0,2:T(8,128)} %copy.78, pred[16,16]{1,0:T(8,128)(4,1)S(1)} %copy-done.5), kind=kOutput, calls=%fused_computation.35 | convolution fusion | flops 50855936 | bytes 4194560 | tf_op jit(solution)/shard_map/tsh,bsh->bth/dot_general | solution.py:80
  290.2 6.1 %copy.85 = f32[2048,8,16]{0,2,1:T(8,128)} copy(f32[2048,8,16]{2,1,0:T(8,128)} %fusion.24) | data formatting | bytes 2097152 | tf_op jit(solution)/shard_map/tsh,bsh->bth/dot_general | solution.py:80
  296.3 27.9 %while.55 = (s32[]{:T(128)}, f32[32,2048]{1,0:T(8,128)}, s32[]{:T(128)}, f32[16,32,2048]{2,1,0:T(8,128)}, f32[16,32,2048]{2,1,0:T(8,128)}, /*index=5*/s32[]{:T(128)}, s32[]{:T(128)}) while((s32[]{:T(128)}, f32[32,2048]{1,0:T(8,128)}, s32[]{:T(128)}, f32[16,32,2048]{2,1,0:T(8,128)}, f32[16,32,2048]{2,1,0:T(8,128)}, ...), condition=%wide.region_6.7_spmd.clone, body=%wide.region_5.6_spmd.clone.sunk | while | flops 262148 | bytes 1048677 | solution.py:20
  296.3 1.8 fusion.98
  298.1 1.9 fusion.98
  300.0 1.9 fusion.98
  301.9 1.9 fusion.98
  303.8 1.9 fusion.98
  305.6 1.9 fusion.98
  307.5 1.9 fusion.98
  309.3 1.9 fusion.98
  311.2 1.9 fusion.98
  313.1 1.9 fusion.98
  314.9 1.9 fusion.98
  316.8 1.9 fusion.98
  318.6 1.9 fusion.98
  320.5 1.9 fusion.98
  322.4 1.9 fusion.98
  324.2 3.6 multiply_add_fusion.1
  327.8 6.4 %copy.84 = f32[8,32,2048]{1,0,2:T(8,128)} copy(f32[8,32,2048]{2,1,0:T(8,128)} %multiply_add_fusion.1) | data formatting | bytes 4194304 | tf_op jit(solution)/shard_map/add | solution.py:82
  334.2 34.1 %fusion.16 = f32[2048,8,16]{2,1,0:T(8,128)} fusion(f32[8,32,2048]{1,0,2:T(8,128)} %copy.84, f32[16]{0:T(128)S(1)} %copy-done.11, f32[32,2048]{0,1:T(8,128)} %copy.83, f32[32,2048]{0,1:T(8,128)S(1)} %copy.76), kind=kOutput, calls=%fused_computation.27 | convolution fusion | flops 102760448 | bytes 3670080 | tf_op jit(solution)/shard_map/tnh,bnh->bth/dot_general | solution.py:83
  368.3 6.1 %copy.86 = f32[2048,8,16]{0,2,1:T(8,128)} copy(f32[2048,8,16]{2,1,0:T(8,128)} %fusion.16) | data formatting | bytes 2097152 | tf_op jit(solution)/shard_map/tnh,bnh->bth/dot_general | solution.py:83
  374.4 3.7 fusion.49
  378.9 4.7 copy.91
  383.5 22.8 %fusion.45 = f32[8,32,2048]{1,0,2:T(8,128)} fusion(f32[8,16,2048]{1,0,2:T(8,128)} %copy.91, f32[32,2048]{0,1:T(8,128)} %copy.92, f32[32,2048]{0,1:T(8,128)S(1)} %copy.88, f32[16]{0:T(128)S(1)} %copy-done.14), kind=kOutput, calls=%fused_computation.55 | convolution fusion | flops 102760448 | bytes 3670080 | tf_op jit(solution)/shard_map/snh,bsh->bnh/dot_general | solution.py:72
  406.3 6.3 %copy.94 = f32[8,32,2048]{2,1,0:T(8,128)} copy(f32[8,32,2048]{1,0,2:T(8,128)} %fusion.45) | data formatting | bytes 4194304
  412.6 1.6 broadcast.473
  414.2 14.7 %while.56 = (s32[]{:T(128)}, f32[32,2048]{1,0:T(8,128)S(1)}, f32[8,32,2048]{2,1,0:T(8,128)}, f32[8,32,2048]{2,1,0:T(8,128)}, f32[32]{0:T(128)S(1)}, /*index=5*/f32[2048]{0:T(1024)S(1)}, s32[]{:T(128)}, s32[]{:T(128)}) while((s32[]{:T(128)}, f32[32,2048]{1,0:T(8,128)S(1)}, f32[8,32,2048]{2,1,0:T(8,128)}, ...), condition=%wide.region_11.12_spmd.clone, body=%wide.region_10.11_spmd.clone.sunk | while | flops 458755 | bytes 1319652 | solution.py:78
  429.6 2.2 copy.95
  431.9 1.5 copy.89
  433.4 2.8 gather_fusion.1
  436.2 12.0 %copy.90 = f32[16,16,2048]{1,0,2:T(8,128)} copy(f32[16,16,2048]{2,1,0:T(8,128)} %bitcast.93) | data formatting | bytes 4194304 | tf_op jit(solution)/shard_map/gather | solution.py:29
  448.2 31.3 %fusion.14 = f32[2048,8,16]{2,1,0:T(8,128)} fusion(f32[8,16,2048]{1,0,2:T(8,128)} %copy.91, f32[16,16,2048]{1,0,2:T(8,128)} %copy.90, pred[16,16]{1,0:T(8,128)(4,1)S(1)} %copy-done.6), kind=kOutput, calls=%fused_computation.24 | convolution fusion | flops 50855936 | bytes 4194560 | tf_op jit(solution)/shard_map/tsh,bsh->bth/dot_general | solution.py:80
  479.5 6.0 %copy.97 = f32[2048,8,16]{0,2,1:T(8,128)} copy(f32[2048,8,16]{2,1,0:T(8,128)} %fusion.14) | data formatting | bytes 2097152 | tf_op jit(solution)/shard_map/tsh,bsh->bth/dot_general | solution.py:80
  485.5 19.1 %while.57 = (s32[]{:T(128)}, f32[32,2048]{1,0:T(8,128)S(1)}, s32[]{:T(128)}, f32[16,32,2048]{2,1,0:T(8,128)}, f32[16,32,2048]{2,1,0:T(8,128)}, /*index=5*/s32[]{:T(128)}, s32[]{:T(128)}) while((s32[]{:T(128)}, f32[32,2048]{1,0:T(8,128)S(1)}, s32[]{:T(128)}, f32[16,32,2048]{2,1,0:T(8,128)}, f32[16,32,2048]{2,1,0:T(8,128)}, ...), condition=%wide.region_13.14_spmd.clone, body=%wide.region_12.13_spmd.clone.sunk | while | flops 262148 | bytes 1048677 | solution.py:20
  486.8 1.3 fusion.99
  490.6 1.3 fusion.99
  493.2 1.3 fusion.99
  499.5 1.3 fusion.99
  504.6 3.5 multiply_add_fusion
  508.1 6.4 %copy.96 = f32[8,32,2048]{1,0,2:T(8,128)} copy(f32[8,32,2048]{2,1,0:T(8,128)} %multiply_add_fusion) | data formatting | bytes 4194304 | tf_op jit(solution)/shard_map/add | solution.py:82
  514.5 34.0 %fusion.6 = f32[2048,8,16]{2,1,0:T(8,128)} fusion(f32[8,32,2048]{1,0,2:T(8,128)} %copy.96, f32[32,2048]{0,1:T(8,128)} %copy.95, f32[32,2048]{0,1:T(8,128)S(1)} %copy.88, f32[16]{0:T(128)S(1)} %copy-done.12), kind=kOutput, calls=%fused_computation.16 | convolution fusion | flops 102760448 | bytes 3670080 | tf_op jit(solution)/shard_map/tnh,bnh->bth/dot_general | solution.py:83
  548.4 6.1 %copy.98 = f32[2048,8,16]{0,2,1:T(8,128)} copy(f32[2048,8,16]{2,1,0:T(8,128)} %fusion.6) | data formatting | bytes 2097152 | tf_op jit(solution)/shard_map/tnh,bnh->bth/dot_general | solution.py:83
  554.5 3.4 fusion.51
  (118 shorter events, 55.3 us)
Async XLA Ops:
  6.5 6.9 %copy-start.4 = (bf16[512,1024]{1,0:T(8,128)(2,1)S(1)}, bf16[512,1024]{1,0:T(8,128)(2,1)}, u32[]{:S(2)}) copy-start(bf16[512,1024]{1,0:T(8,128)(2,1)} %param.14) | copy-start | bytes 3145732
  6.5 8.4 %copy-start.9 = (f32[2,2048]{1,0:T(2,128)S(1)}, f32[2,2048]{1,0:T(2,128)}, u32[]{:S(2)}) copy-start(f32[2,2048]{1,0:T(2,128)} %param.16) | copy-start | bytes 49156
  6.5 132.1 %all-gather.8.cloned.1.call-start = ((), (), s32[]{:S(2)}) async-start(), calls=%async_computation | async-start | bytes 17825792 | tf_op jit(solution)/shard_map/all_gather | solution.py:92
  7.3 289.1 %all-gather.10.cloned.1.call-start = ((), (), s32[]{:S(2)}) async-start(), calls=%async_computation.1 | async-start | bytes 4456448 | tf_op jit(solution)/shard_map/all_gather | solution.py:11
  10.5 285.8 %all-gather.14.cloned.1.call-start = ((), (), s32[]{:S(2)}) async-start(), calls=%async_computation.3 | async-start | bytes 4456448 | tf_op jit(solution)/shard_map/all_gather | solution.py:11
  11.8 142.9 %copy-start.13 = (f32[16]{0:T(128)}, f32[16]{0:T(128)S(1)}, u32[]{:S(2)}) copy-start(f32[16]{0:T(128)S(1)} %subtract_negate_fusion) | copy-start | bytes 196
  200.1 0.7 copy-start.1
  200.8 284.7 %all-gather.12.cloned.1.call-start = ((), (), s32[]{:S(2)}) async-start(), calls=%async_computation.2 | async-start | bytes 4456448 | tf_op jit(solution)/shard_map/all_gather | solution.py:11
  201.4 284.1 %all-gather.16.cloned.1.call-start = ((), (), s32[]{:S(2)}) async-start(), calls=%async_computation.4 | async-start | bytes 4456448 | tf_op jit(solution)/shard_map/all_gather | solution.py:11
  244.0 12.0 %copy-start.10 = (f32[2,2048]{1,0:T(2,128)S(1)}, f32[2,2048]{1,0:T(2,128)}, u32[]{:S(2)}) copy-start(f32[2,2048]{1,0:T(2,128)} %param.19) | copy-start | bytes 49156
  244.0 14.9 %copy-start.5 = (pred[16,16]{1,0:T(8,128)(4,1)S(1)}, pred[16,16]{1,0:T(8,128)(4,1)}, u32[]{:S(2)}) copy-start(pred[16,16]{1,0:T(8,128)(4,1)} %subtract_compare_fusion) | copy-start | bytes 772
  290.2 34.0 %copy-start.15 = (f32[8]{0:T(128)S(1)}, f32[8]{0:T(128)}, u32[]{:S(2)}) copy-start(f32[8]{0:T(128)} %iota_multiply_fusion) | copy-start | bytes 100
  324.2 10.0 %copy-start.11 = (f32[16]{0:T(128)S(1)}, f32[16]{0:T(128)}, u32[]{:S(2)}) copy-start(f32[16]{0:T(128)} %add_negate_fusion) | copy-start | bytes 196
  368.3 6.1 %copy-start.2 = (f32[128,2048]{1,0:T(8,128)S(1)}, f32[128,2048]{1,0:T(8,128)}, u32[]{:S(2)}) copy-start(f32[128,2048]{1,0:T(8,128)} %multiply_multiply_fusion.11) | copy-start | bytes 3145732
  368.3 10.3 %copy-start.8 = (f32[1,2048]{1,0:T(1,128)S(1)}, f32[1,2048]{1,0:T(1,128)}, u32[]{:S(2)}) copy-start(f32[1,2048]{1,0:T(1,128)} %get-tuple-element.445) | copy-start | bytes 24580
  378.1 5.4 copy-start.14
  428.9 0.7 copy-start
  436.2 12.0 %copy-start.6 = (pred[16,16]{1,0:T(8,128)(4,1)S(1)}, pred[16,16]{1,0:T(8,128)(4,1)}, u32[]{:S(2)}) copy-start(pred[16,16]{1,0:T(8,128)(4,1)} %subtract_compare_fusion) | copy-start | bytes 772
  479.5 25.1 %copy-start.16 = (f32[8]{0:T(128)S(1)}, f32[8]{0:T(128)}, u32[]{:S(2)}) copy-start(f32[8]{0:T(128)} %iota_multiply_fusion) | copy-start | bytes 100
  504.6 9.9 %copy-start.12 = (f32[16]{0:T(128)S(1)}, f32[16]{0:T(128)}, u32[]{:S(2)}) copy-start(f32[16]{0:T(128)} %add_negate_fusion) | copy-start | bytes 196
  548.4 6.1 %copy-start.3 = (f32[2048,8,16]{0,2,1:T(8,128)S(1)}, f32[2048,8,16]{0,2,1:T(8,128)}, u32[]{:S(2)}) copy-start(f32[2048,8,16]{0,2,1:T(8,128)} %copy.97) | copy-start | bytes 3145732
  548.4 6.1 %copy-start.7 = (f32[1,2048]{1,0:T(1,128)S(1)}, f32[1,2048]{1,0:T(1,128)}, u32[]{:S(2)}) copy-start(f32[1,2048]{1,0:T(1,128)} %get-tuple-element.443) | copy-start | bytes 24580
Sparse Core Ops, SparseCore 0:
  9.5 129.1 all-gather.7
  140.8 48.5 all-gather.9
  200.9 48.7 all-gather.13
  251.7 48.8 all-gather.11
  429.7 48.7 all-gather.15
where the time goes:
time: 577 us; the launch traced here: 566 us
  matrix products  185 us (32%)
  other arithmetic  126 us (22%)
  waiting for transfers between devices  124 us (21%)
  local copies, waits for them, and re-layouts  116 us (20%)
  between operations  13.8 us (2%)
    all_gather x1, waiting for transfers between devices, local(): full_weight = lax.all_gather(pool_weight, 'tm', axis=0, tiled=True)  123 us
    dot_general x2, matrix products, state_layer(): carried = jnp.einsum('tnh,bnh->bth', outof_table, full_in, precision=exact)  68.1 us
    dot_general x2, matrix products, state_layer(): inner = jnp.einsum('tsh,bsh->bth', toeplitz, grouped, precision=exact)  62.7 us
    select_n x30, other arithmetic, turn(): jnp.where(position < mine, new, old)  46.6 us
    dot_general x2, matrix products, state_layer(): jnp.einsum('snh,bsh->bnh', into_table, grouped, precision=exact)  45.6 us
    gather x4, local copies, waits for them, and re-layouts, build_tables(): picked = kernel[jnp.clip(lag_gap, 0, block_len - 1)]  29.5 us
    reduce_sum x1, other arithmetic, build_tables(): kernel = jnp.sum(out_mix[None] * in_scale[None] * powers, axis=1)  26.7 us
    add x16, other arithmetic, advance(): return (block_decay * state + block_end, state)  17.4 us
  transfers between devices with their start and end apart: 5, of which 1 were waited for; matrix products, arithmetic and copies ran while one was open for 62% of the time, Pallas kernels for 0%

commit v1 on v0

v1 whole, which is shorter than its diff:
```python
import functools

import jax
import jax.numpy as jnp
from jax import lax
from jax.experimental import pallas as pl
from jax.experimental.pallas import tpu as pltpu
from jax.sharding import PartitionSpec as P

POOL = 4
SPLIT = 4
BLOCK = 16
LANES = 128


def block_ends(x_ref, decay_ref, ends_ref, modes, cols):
    rows = x_ref.shape[0]
    blocks = rows // BLOCK
    span = 8 * BLOCK

    def group(g, carry):
        base = pl.multiple_of(g * span, span)
        xs = [x_ref[pl.ds(base + j, 8, stride=BLOCK), cols] for j in range(BLOCK)]
        for n in range(modes):
            decay = jnp.broadcast_to(decay_ref[pl.ds(n, 1), cols], (8, LANES))
            end = xs[0]
            for j in range(1, BLOCK):
                end = end * decay + xs[j]
            ends_ref[pl.ds(pl.multiple_of(n * blocks + g * 8, 8), 8), cols] = end
        return carry

    lax.fori_loop(0, rows // span, group, 0)


def scan_blocks(ends_ref, step_ref, modes, cols, start, out_ref=None):
    blocks = ends_ref.shape[0] // modes
    groups = modes // 8
    steps = [step_ref[pl.ds(i * 8, 8), cols] for i in range(groups)]
    outs = [out_ref[pl.ds(i * 8, 8), cols] for i in range(groups)] if out_ref is not None else None
    states = list(start)
    for b in range(blocks):
        for i in range(groups):
            where = pl.ds(i * 8 * blocks + b, 8, stride=blocks)
            end = ends_ref[where, cols]
            if outs is not None:
                ends_ref[where, cols] = states[i] * outs[i]
            states[i] = states[i] * steps[i] + end
    return states


def respond(x_ref, hidden_ref, ends_ref, powers_ref, kernel_ref, result_ref, modes, cols):
    rows = x_ref.shape[0]
    blocks = rows // BLOCK
    span = 8 * BLOCK

    def group(g, carry):
        base = pl.multiple_of(g * span, span)
        coefs = [
            ends_ref[pl.ds(pl.multiple_of(n * blocks + g * 8, 8), 8), cols] for n in range(modes)
        ]
        xs = [x_ref[pl.ds(base + j, 8, stride=BLOCK), cols] for j in range(BLOCK)]
        for j in range(BLOCK):
            power = jnp.broadcast_to(powers_ref[pl.ds(j, 1), cols], (8, LANES))
            total = coefs[modes - 1]
            for n in range(modes - 2, -1, -1):
                total = total * power + coefs[n]
            total = total * power
            for i in range(j + 1):
                total = total + xs[i] * jnp.broadcast_to(
                    kernel_ref[pl.ds(j - i, 1), cols], (8, LANES)
                )
            where = pl.ds(base + j, 8, stride=BLOCK)
            gelu = 0.5 * total * (1.0 + lax.erf(total * 0.7071067811865476))
            result_ref[where, cols] = hidden_ref[where, cols] + gelu
        return carry

    lax.fori_loop(0, rows // span, group, 0)


def ends_kernel(modes, x_ref, decay_ref, step_ref, ends_ref, last_ref):
    cols = slice(None)
    block_ends(x_ref, decay_ref, ends_ref, modes, cols)
    zero = [jnp.zeros((8, LANES), jnp.float32)] * (modes // 8)
    last = scan_blocks(ends_ref, step_ref, modes, cols, zero)
    for i in range(modes // 8):
        last_ref[pl.ds(i * 8, 8), cols] = last[i]


def respond_kernel(
    modes, x_ref, hidden_ref, ends_in_ref, start_ref, step_ref, out_ref, powers_ref, kernel_ref,
    result_ref, ends_ref
):
    cols = slice(None)
    ends_ref[...] = ends_in_ref[...]
    start = [start_ref[pl.ds(i * 8, 8), cols] for i in range(modes // 8)]
    scan_blocks(ends_ref, step_ref, modes, cols, start, out_ref)
    respond(x_ref, hidden_ref, ends_ref, powers_ref, kernel_ref, result_ref, modes, cols)


def by_lanes(rows):
    return pl.BlockSpec((rows, LANES), lambda i: (0, i))


def tables(step_row, out_mix, skip_row, rows):
    modes = out_mix.shape[0]
    rates = step_row[None, :] * (jnp.arange(modes, dtype=jnp.float32) + 1.0)[:, None]
    in_scale = jnp.sqrt(-jnp.expm1(-2.0 * rates))
    out = out_mix * in_scale
    lags = jnp.arange(BLOCK, dtype=jnp.float32)
    kernel = jnp.sum(out[None] * jnp.exp(-lags[:, None, None] * rates[None]), axis=1)
    kernel = kernel.at[0].add(skip_row)
    powers = jnp.exp(-(lags + 1.0)[:, None] * step_row[None, :])
    return {
        "decay": jnp.exp(-rates),
        "step": jnp.exp(-rates * BLOCK),
        "whole": jnp.exp(-rates * rows),
        "out": out,
        "powers": powers,
        "kernel": kernel,
    }


def state_layer(hidden, gain, table, low_groups, high_groups):
    rows, chans = hidden.shape
    modes = table["decay"].shape[0]
    blocks = rows // BLOCK
    mean = jnp.mean(hidden, axis=-1)
    spread = jnp.sum(jnp.square(hidden - mean[:, None]), axis=-1)
    stats = lax.all_gather(jnp.stack([mean, spread]), "tm", axis_index_groups=low_groups)
    row_mean = jnp.mean(stats[:, 0], axis=0)
    row_var = (
        jnp.sum(stats[:, 1], axis=0) + chans * jnp.sum(jnp.square(stats[:, 0] - row_mean), axis=0)
    ) / (chans * SPLIT)
    normed = (hidden - row_mean[:, None]) * lax.rsqrt(row_var + 1e-05)[:, None] * gain[None, :]
    grid = (chans // LANES,)
    ends, last = pl.pallas_call(
        functools.partial(ends_kernel, modes),
        grid=grid,
        in_specs=[by_lanes(rows), by_lanes(modes), by_lanes(modes)],
        out_specs=[by_lanes(modes * blocks), by_lanes(modes)],
        out_shape=[
            jax.ShapeDtypeStruct((modes * blocks, chans), jnp.float32),
            jax.ShapeDtypeStruct((modes, chans), jnp.float32),
        ],
    )(normed, table["decay"], table["step"])
    every = lax.all_gather(last, "tm", axis_index_groups=high_groups)
    mine = lax.axis_index("tm") // SPLIT
    start = jnp.zeros_like(last)
    for p in range(len(high_groups[0]) - 1):
        start = jnp.where(p < mine, table["whole"] * start + every[p], start)
    return pl.pallas_call(
        functools.partial(respond_kernel, modes),
        grid=grid,
        in_specs=[
            by_lanes(rows), by_lanes(rows), by_lanes(modes * blocks), by_lanes(modes),
            by_lanes(modes), by_lanes(modes), by_lanes(BLOCK), by_lanes(BLOCK),
        ],
        out_specs=by_lanes(rows),
        out_shape=jax.ShapeDtypeStruct((rows, chans), jnp.float32),
        scratch_shapes=[pltpu.VMEM((modes * blocks, LANES), jnp.float32)],
    )(normed, hidden, ends, start, table["step"], table["out"], table["powers"], table["kernel"])


def local(signal, pool_weight, norm_gain, step_size, mode_out, skip_gain):
    fine_rows, channels = signal.shape
    count = lax.axis_size("tm")
    low = lax.axis_index("tm") % SPLIT
    low_groups = [[h * SPLIT + i for i in range(SPLIT)] for h in range(count // SPLIT)]
    high_groups = [[h * SPLIT + i for h in range(count // SPLIT)] for i in range(SPLIT)]
    coarse = signal.reshape(fine_rows // POOL, POOL * channels)
    coarse = lax.all_gather(coarse, "tm", axis_index_groups=low_groups, axis=0, tiled=True)
    weight = lax.all_to_all(
        pool_weight, "tm", 1, 0, axis_index_groups=low_groups, tiled=True
    )
    weight = lax.all_gather(weight, "tm", axis_index_groups=high_groups, axis=0, tiled=True)
    hidden = jnp.dot(coarse, weight, preferred_element_type=jnp.float32)
    rows, chans = hidden.shape

    def own(array):
        return lax.dynamic_slice_in_dim(array, low * chans, chans, axis=array.ndim - 1)

    gain, step, mix, skip = own(norm_gain), own(step_size), own(mode_out), own(skip_gain)
    for l in range(norm_gain.shape[0]):
        table = tables(step[l], mix[l], skip[l], rows)
        hidden = state_layer(hidden, gain[l], table, low_groups, high_groups)
    return lax.all_to_all(
        hidden.astype(jnp.bfloat16), "tm", 0, 1, axis_index_groups=low_groups, tiled=True
    )


def solution(mesh):
    placed = (P(("parts", "tm"), None), P("tm", None), P(), P(), P(), P())
    return jax.shard_map(
        local, mesh=mesh, in_specs=placed, out_specs=P(("parts", "tm"), None), check_vma=False
    )
```

time: 577 us -> 239 us (0.41); the launches traced: 566 us -> 238 us
  matrix products: 185 us -> 5.85 us
  other arithmetic: 126 us -> 12.7 us
  local copies, waits for them, and re-layouts: 116 us -> 7.52 us
  blocking collectives: 0 us -> 76.9 us
  waiting for transfers between devices: 124 us -> 93.9 us
  Pallas kernels: 0 us -> 27.8 us
    dot_general x7 -> x1, matrix products: 185 us -> 5.85 us  [local(): hidden = jnp.dot(coarse, weight, preferred_element_type=jnp.float32)]
    select_n x31 -> x2, other arithmetic: 47.2 us -> 1.45 us  [state_layer(): start = jnp.where(p < mine, table['whole'] * start + every[p], start)]
    all_gather x0 -> x4, blocking collectives: none -> 39.9 us  [the longest x2 29.5 us: state_layer(): every = lax.all_gather(last, 'tm', axis_index_groups=high_groups)]
    all_to_all x0 -> x2, blocking collectives: none -> 37.1 us  [the longest x1 25.8 us: local(): lax.all_to_all(pool_weight, 'tm', 1, 0, axis_index_groups=low_groups, til...]
    gather x4 -> x0, local copies, waits for them, and re-layouts: 29.5 us -> none  [build_tables(): picked = kernel[jnp.clip(lag_gap, 0, block_len - 1)]]
    all_gather x5 -> x2, waiting for transfers between devices: 123 us -> 93.9 us  [the longest x1 82.7 us: local(): lax.all_gather(weight, 'tm', axis_index_groups=high_groups, axis=0, tiled...]
    pallas_call x0 -> x4, Pallas kernels: none -> 27.8 us  [the longest x2 17.3 us: state_layer(): pl.pallas_call(functools.partial(respond_kernel, modes), grid=grid, in_sp...]
    dot_general x4 -> x1, local copies, waits for them, and re-layouts: 24.3 us -> 0.33 us  [local(): hidden = jnp.dot(coarse, weight, preferred_element_type=jnp.float32)]
  transfers between devices with their start and end apart: 5 -> 2, of which waited for: 1 -> 2; matrix products, arithmetic and copies ran while one was open for 62% -> 3% of each run, Pallas kernels for 0% -> 0%
where the time goes in v1:
time: 239 us; the launch traced here: 238 us
  waiting for transfers between devices  93.9 us (39%)
  blocking collectives  76.9 us (32%)
  Pallas kernels  27.8 us (12%)
  between operations  13.6 us (6%)
  other arithmetic  12.7 us (5%)
  local copies, waits for them, and re-layouts  7.52 us (3%)
  matrix products  5.85 us (2%)
    all_gather x1, waiting for transfers between devices, local(): lax.all_gather(weight, 'tm', axis_index_groups=high_groups, axis=0, tiled...  82.7 us
    all_gather x2, blocking collectives, state_layer(): every = lax.all_gather(last, 'tm', axis_index_groups=high_groups)  29.5 us
    all_to_all x1, blocking collectives, local(): lax.all_to_all(pool_weight, 'tm', 1, 0, axis_index_groups=low_groups, til...  25.8 us
    pallas_call x2, Pallas kernels, state_layer(): pl.pallas_call(functools.partial(respond_kernel, modes), grid=grid, in_sp...  17.3 us
    all_to_all x1, blocking collectives, local(): lax.all_to_all(hidden.astype(jnp.bfloat16), 'tm', 0, 1, axis_index_groups...  11.3 us
    all_gather x1, waiting for transfers between devices, local(): lax.all_gather(coarse, 'tm', axis_index_groups=low_groups, axis=0, tiled=...  11.3 us
    pallas_call x2, Pallas kernels, state_layer(): pl.pallas_call(functools.partial(ends_kernel, modes), grid=grid, in_specs...  10.5 us
    all_gather x2, blocking collectives, state_layer(): lax.all_gather(jnp.stack([mean, spread]), 'tm', axis_index_groups=low_gro...  10.4 us
  transfers between devices with their start and end apart: 2, of which 2 were waited for; matrix products, arithmetic and copies ran while one was open for 3% of the time, Pallas kernels for 0%

profile of v1, /device:TPU:0, one launch (start us, length us, event | category | flops | bytes accessed | tf_op | source)
XLA Modules:
  0.0 238.3 jit_solution(12732408027454425490)
XLA Ops:
  6.5 0.0 all-gather.9.cloned.1.call-start
  6.5 2.6 %reshape.297 = bf16[128,4096]{1,0:T(8,128)(2,1)} reshape(bf16[512,1024]{1,0:T(8,128)(2,1)} %param.10) | data formatting | bytes 2097152 | tf_op jit(solution)/shard_map/reshape | solution.py:170
  9.1 0.0 copy-start.1
  9.1 0.0 all-gather.9.cloned.1.call-update
  9.1 0.0 all-gather.11.cloned.1.call-start
  9.2 1.5 copy.23
  10.7 25.8 %all_to_all.38 = bf16[256,4,512]{0,2,1:T(8,128)(2,1)S(1)} all-to-all(bf16[256,4,512]{0,2,1:T(8,128)(2,1)S(1)} %bitcast.43), channel_id=1, replica_groups={{0,1,2,3},{4,5,6,7},{8,9,10,11},{12,13,14,15},{16,17,18,19},{20,21,22,2..., dimensions={1} | all-to-all | bytes 2097152 | tf_op jit(solution)/shard_map/all_to_all | solution.py:172
  36.5 1.3 copy.24
  37.8 0.0 all-gather.11.cloned.1.call-update
  37.9 0.8 fusion.11
  38.7 0.0 copy-done.1
  38.7 0.2 multiply_bitcast_fusion.1
  38.9 0.9 bitcast_multiply_fusion
  39.8 0.5 multiply_reduce_fusion
  40.3 0.9 dynamic-slice_add_fusion
  41.2 0.0 copy-start.3
  41.2 0.1 scatter-add.9.kernel_ref
  41.3 0.0 copy-start.2
  41.3 0.7 multiply_exponential_fusion.2
  42.0 11.3 %all-gather.9.cloned.1.call-done = bf16[512,4096]{1,0:T(8,128)(2,1)} async-done(((bf16[128,4096]{1,0:T(8,128)(2,1)}), bf16[512,4096]{1,0:T(8,128)(2,1)}) %all-gather.9.cloned.1.call-update) | async-done | bytes 4194320 | tf_op jit(solution)/shard_map/all_gather | solution.py:171
  53.3 82.7 %all-gather.11.cloned.1.call-done = bf16[4096,512]{1,0:T(8,128)(2,1)} async-done(((bf16[1024,512]{1,0:T(8,128)(2,1)}), bf16[4096,512]{1,0:T(8,128)(2,1)}) %all-gather.11.cloned.1.call-update) | async-done | bytes 4194320 | tf_op jit(solution)/shard_map/all_gather | solution.py:175
  135.9 5.9 %fusion.12 = (f32[512]{0:T(512)S(1)}, f32[512,512]{0,1:T(8,128)S(1)}) fusion(bf16[512,4096]{1,0:T(8,128)(2,1)} %all-gather.9.cloned.1.call-done, bf16[4096,512]{1,0:T(8,128)(2,1)} %all-gather.11.cloned.1.call-done), kind=kOutput, calls=%fused_computation.57 | convolution fusion | flops 2147745280 | bytes 9439232 | tf_op jit(solution)/shard_map/dot_general | solution.py:176
  141.8 0.0 copy-done.3
  141.8 0.0 copy-done.2
  141.8 0.3 copy.25.hidden_ref
  142.1 0.0 copy-start
  142.1 0.2 multiply_reduce_fusion.3
  142.3 5.2 %all-gather.4 = f32[4,2,512]{2,1,0:T(2,128)S(1)} all-gather(f32[1,2,512]{2,1,0:T(2,128)S(1)} %maximum_bitcast_fusion), channel_id=2, replica_groups={{0,1,2,3},{4,5,6,7},{8,9,10,11},{12,13,14,15},{16,17,18,19},{20,21,22,2..., dimensions={0}, use_global_device_ids=true | all-gather | bytes 20480 | tf_op jit(solution)/shard_map/all_gather | solution.py:129
  147.6 1.2 multiply_multiply_fusion.1.x_ref
  148.8 5.2 %shard_map.64 = (f32[1024,512]{1,0:T(8,128)}, f32[32,512]{1,0:T(8,128)}) custom-call(f32[512,512]{1,0:T(8,128)} %multiply_multiply_fusion.1.x_ref, f32[32,512]{1,0:T(8,128)} %get-tuple-element.56.decay_ref, f32[32,512]{1,0:T(8,128)} %get-tuple-element.55.step_ref), custom_call_target="tpu_custom_call" | custom-call | tf_op jit(solution)/shard_map/pallas_call | solution.py:136
  154.1 14.7 %all-gather.1 = f32[128,512]{1,0:T(8,128)S(1)} all-gather(f32[32,512]{1,0:T(8,128)} %get-tuple-element.34), channel_id=3, replica_groups={{0,4,8,12},{1,5,9,13},{2,6,10,14},{3,7,11,15},{16,20,24,28},{17,21,25,2..., dimensions={0}, use_global_device_ids=true | all-gather | bytes 327680 | tf_op jit(solution)/shard_map/all_gather | solution.py:146
  168.8 0.7 fusion.3.start_ref
  169.5 0.0 copy-done
  169.5 8.7 %shard_map.65.hidden_ref = f32[512,512]{1,0:T(8,128)} custom-call(f32[512,512]{1,0:T(8,128)} %multiply_multiply_fusion.1.x_ref, f32[512,512]{1,0:T(8,128)} %copy-done, f32[1024,512]{1,0:T(8,128)} %get-tuple-element.33.ends_in_ref, f32[32,512]{1,0:T(8,128)} %fusion.3.start_ref, f32[32,512]{1,0:T(8,128)} %get-tuple-element.55.step_ref, ...), custom_call_target="tpu_custom_call" | custom-call | tf_op jit(solution)/shard_map/pallas_call | solution.py:151
  178.2 1.4 reduce_sum.114
  179.5 1.5 multiply_reduce_fusion.1
  181.0 5.2 %all-gather.5 = f32[4,2,512]{2,1,0:T(2,128)S(1)} all-gather(f32[1,2,512]{2,1,0:T(2,128)S(1)} %maximum_bitcast_fusion.1), channel_id=4, replica_groups={{0,1,2,3},{4,5,6,7},{8,9,10,11},{12,13,14,15},{16,17,18,19},{20,21,22,2..., dimensions={0}, use_global_device_ids=true | all-gather | bytes 20480 | tf_op jit(solution)/shard_map/all_gather | solution.py:129
  186.3 2.4 %multiply_multiply_fusion.x_ref = f32[512,512]{1,0:T(8,128)} fusion(f32[512,512]{1,0:T(8,128)} %shard_map.65.hidden_ref, f32[512]{0:T(512)S(1)} %bitcast.58, f32[512]{0:T(512)S(1)} %add_rsqrt_fusion, f32[512]{0:T(512)S(1)} %broadcast_multiply_fusion.2), kind=kLoop, calls=%fused_computation.1 | loop fusion | flops 786432 | bytes 2103296 | tf_op jit(solution)/shard_map/mul | solution.py:134
  188.7 5.2 %shard_map.66 = (f32[1024,512]{1,0:T(8,128)}, f32[32,512]{1,0:T(8,128)}) custom-call(f32[512,512]{1,0:T(8,128)} %multiply_multiply_fusion.x_ref, f32[32,512]{1,0:T(8,128)} %get-tuple-element.59.decay_ref, f32[32,512]{1,0:T(8,128)} %get-tuple-element.58.step_ref), custom_call_target="tpu_custom_call" | custom-call | tf_op jit(solution)/shard_map/pallas_call | solution.py:136
  194.0 14.7 %all-gather.3 = f32[128,512]{1,0:T(8,128)S(1)} all-gather(f32[32,512]{1,0:T(8,128)} %get-tuple-element.36), channel_id=5, replica_groups={{0,4,8,12},{1,5,9,13},{2,6,10,14},{3,7,11,15},{16,20,24,28},{17,21,25,2..., dimensions={0}, use_global_device_ids=true | all-gather | bytes 327680 | tf_op jit(solution)/shard_map/all_gather | solution.py:146
  208.7 0.7 fusion.start_ref
  209.4 8.7 %shard_map.67 = f32[512,512]{1,0:T(8,128)} custom-call(f32[512,512]{1,0:T(8,128)} %multiply_multiply_fusion.x_ref, f32[512,512]{1,0:T(8,128)} %shard_map.65.hidden_ref, f32[1024,512]{1,0:T(8,128)} %get-tuple-element.35.ends_in_ref, f32[32,512]{1,0:T(8,128)} %fusion.start_ref, f32[32,512]{1,0:T(8,128)} %get-tuple-element.58.step_ref, ...), custom_call_target="tpu_custom_call" | custom-call | tf_op jit(solution)/shard_map/pallas_call | solution.py:151
  218.1 1.3 convert_element_type.3
  219.4 11.3 %all_to_all.39 = bf16[4,128,512]{2,1,0:T(8,128)(2,1)S(1)} all-to-all(bf16[4,128,512]{2,1,0:T(8,128)(2,1)S(1)} %bitcast.44), channel_id=1, replica_groups={{0,1,2,3},{4,5,6,7},{8,9,10,11},{12,13,14,15},{16,17,18,19},{20,21,22,2..., dimensions={0} | all-to-all | bytes 1048576 | tf_op jit(solution)/shard_map/all_to_all | solution.py:186
  230.7 0.8 copy.30
  (16 shorter events, 0.2 us)
Async XLA Ops:
  6.5 46.7 %all-gather.9.cloned.1.call-start = ((), (), s32[]{:S(2)}) async-start(), calls=%async_computation.2 | async-start | bytes 5242880 | tf_op jit(solution)/shard_map/all_gather | solution.py:171
  9.1 29.6 %copy-start.1 = (f32[2,32,2048]{2,1,0:T(8,128)S(1)}, f32[2,32,2048]{2,1,0:T(8,128)}, u32[]{:S(2)}) copy-start(f32[2,32,2048]{2,1,0:T(8,128)} %param.14) | copy-start | bytes 1572868
  9.1 126.8 %all-gather.11.cloned.1.call-start = ((), (), s32[]{:S(2)}) async-start(), calls=%async_computation.3 | async-start | bytes 5242880 | tf_op jit(solution)/shard_map/all_gather | solution.py:175
  41.2 100.6 %copy-start.3 = (f32[16,512]{1,0:T(8,128)}, f32[16,512]{1,0:T(8,128)S(1)}, u32[]{:S(2)}) copy-start(f32[16,512]{1,0:T(8,128)S(1)} %scatter-add.6.kernel_ref) | copy-start | bytes 98308
  41.3 100.5 %copy-start.2 = (f32[16,512]{1,0:T(8,128)}, f32[16,512]{1,0:T(8,128)S(1)}, u32[]{:S(2)}) copy-start(f32[16,512]{1,0:T(8,128)S(1)} %scatter-add.9.kernel_ref) | copy-start | bytes 98308
  142.1 27.4 %copy-start = (f32[512,512]{1,0:T(8,128)}, f32[512,512]{1,0:T(8,128)S(1)}, u32[]{:S(2)}) copy-start(f32[512,512]{1,0:T(8,128)S(1)} %copy.25.hidden_ref) | copy-start | bytes 3145732
Sparse Core Ops, SparseCore 0:
  9.2 43.9 all-gather.8
  54.8 81.0 all-gather.10

commit v2 on v1

--- a/solution.py
+++ b/solution.py
@@ -11,6 +11,7 @@
 SPLIT = 4
 BLOCK = 16
 LANES = 128
+PIECES = 4
 
 
 def block_ends(x_ref, decay_ref, ends_ref, modes, cols):
@@ -95,6 +96,223 @@
     start = [start_ref[pl.ds(i * 8, 8), cols] for i in range(modes // 8)]
     scan_blocks(ends_ref, step_ref, modes, cols, start, out_ref)
     respond(x_ref, hidden_ref, ends_ref, powers_ref, kernel_ref, result_ref, modes, cols)
+
+
+MESH = pl.DeviceIdType.MESH
+
+
+def pool_kernel(highs, coarse_ref, weight_ref, hidden_ref, all_ref, cols_ref, sems):
+    part, place = lax.axis_index("parts"), lax.axis_index("tm")
+    high, low = place // SPLIT, place % SPLIT
+    depth, width = weight_ref.shape[0], cols_ref.shape[1]
+    half = depth // 2
+    rows = coarse_ref.shape[0]
+    piece = rows // PIECES
+    chunk = SPLIT * depth
+    other = 1 - part
+    (near_send, near_recv, own_sem, line_send, line_recv, side_send, side_recv,
+     rows_send, rows_recv) = sems
+    flip = lambda bit: low + bit - 2 * bit * ((low // bit) % 2)
+    core, cross = flip(1), flip(2)
+    diagonal = SPLIT - 1 - low
+    at = lambda p, h, l: (p, h * SPLIT + l)
+
+    barrier = pltpu.get_barrier_semaphore()
+
+    def greet(device):
+        pl.semaphore_signal(barrier, inc=1, device_id=device, device_id_type=MESH)
+
+    for who in (core, cross, diagonal):
+        greet(at(part, high, who))
+    greet(at(other, high, low))
+    pl.when(high > 0)(lambda: greet(at(part, high - 1, low)))
+    pl.when(high < highs - 1)(lambda: greet(at(part, high + 1, low)))
+
+    def spot(h, l, which):
+        start = pl.multiple_of(h * chunk + l * depth + which * half, half)
+        return cols_ref.at[pl.ds(start, half), :]
+
+    def near(bit, which):
+        to = (core, cross, diagonal)[bit]
+        mine = weight_ref.at[
+            pl.ds(pl.multiple_of(which * half, half), half),
+            pl.ds(pl.multiple_of(to * width, width), width),
+        ]
+        return pltpu.make_async_remote_copy(
+            mine, spot(high, low, which), near_send.at[bit, which], near_recv.at[bit, which],
+            device_id=at(part, high, to), device_id_type=MESH,
+        )
+
+    def near_arrived(bit, which):
+        who = (core, cross, diagonal)[bit]
+        pltpu.make_async_remote_copy(
+            spot(high, who, which), spot(high, who, which), near_send.at[bit, which],
+            near_recv.at[bit, which], device_id=at(part, high, who), device_id_type=MESH,
+        ).wait_recv()
+
+    def line(up, h, l):
+        to = jnp.clip(high + (1 if up else -1), 0, highs - 1)
+        return pltpu.make_async_remote_copy(
+            spot(h, l, part), spot(h, l, part), line_send.at[int(up), h, l], line_recv.at[h, l],
+            device_id=at(part, to, low), device_id_type=MESH,
+        )
+
+    def side(h, l, which):
+        return pltpu.make_async_remote_copy(
+            spot(h, l, which), spot(h, l, which), side_send.at[h, l], side_recv.at[h, l],
+            device_id=at(other, high, low), device_id_type=MESH,
+        )
+
+    def block(owner, p):
+        start = pl.multiple_of(owner * rows + p * piece, piece)
+        return all_ref.at[pl.ds(start, piece), :]
+
+    def give(bit, p):
+        to = core if bit == 0 else cross
+        return pltpu.make_async_remote_copy(
+            coarse_ref.at[pl.ds(p * piece, piece), :], block(low, p), rows_send.at[bit, p],
+            rows_recv.at[bit, p], device_id=at(part, high, to), device_id_type=MESH,
+        )
+
+    def taken(bit, p):
+        who = (core, cross, diagonal)[bit]
+        pltpu.make_async_remote_copy(
+            block(who, p), block(who, p), rows_send.at[bit, p], rows_recv.at[bit, p],
+            device_id=at(part, high, core), device_id_type=MESH,
+        ).wait_recv()
+
+    def pass_on(p):
+        return pltpu.make_async_remote_copy(
+            block(cross, p), block(cross, p), rows_send.at[2, p], rows_recv.at[2, p],
+            device_id=at(part, high, core), device_id_type=MESH,
+        )
+
+    own_weight = pltpu.make_async_copy(
+        weight_ref.at[:, pl.ds(pl.multiple_of(low * width, width), width)],
+        cols_ref.at[pl.ds(pl.multiple_of(high * chunk + low * depth, depth), depth), :],
+        own_sem.at[0],
+    )
+    own_rows = pltpu.make_async_copy(
+        coarse_ref, all_ref.at[pl.ds(pl.multiple_of(low * rows, rows), rows), :], own_sem.at[1]
+    )
+    own_weight.start()
+    own_rows.start()
+    ahead = jnp.minimum(high, 1) + jnp.minimum(highs - 1 - high, 1)
+    pl.semaphore_wait(barrier, 4 + ahead)
+
+    for bit in (1, 2, 0):
+        near(bit, part).start()
+    for p in range(PIECES):
+        give(1, p).start()
+    for p in range(PIECES):
+        give(0, p).start()
+    for bit in (1, 2, 0):
+        near(bit, other).start()
+
+    def both_ways(h, l):
+        pl.when(high < highs - 1)(lambda: line(True, h, l).start())
+        pl.when(high > 0)(lambda: line(False, h, l).start())
+
+    own_weight.wait()
+    both_ways(high, low)
+    for bit, who in ((0, core), (1, cross), (2, diagonal)):
+        near_arrived(bit, part)
+        both_ways(high, who)
+
+    def step(s, carry):
+        for l in range(SPLIT):
+            @pl.when(high - s >= 0)
+            def _():
+                h = high - s
+                line(True, h, l).wait_recv()
+                pl.when(high < highs - 1)(lambda: line(True, h, l).start())
+                side(h, l, part).start()
+
+            @pl.when(high + s < highs)
+            def _():
+                h = high + s
+                line(False, h, l).wait_recv()
+                pl.when(high > 0)(lambda: line(False, h, l).start())
+                side(h, l, part).start()
+
+        @pl.when(s < PIECES)
+        def _():
+            taken(1, s - 1)
+            pass_on(s - 1).start()
+
+        return carry
+
+    lax.fori_loop(1, highs, step, 0)
+    for p in range(min(PIECES - 1, highs - 1), PIECES):
+        taken(1, p)
+        pass_on(p).start()
+    own_rows.wait()
+    for p in range(PIECES):
+        taken(0, p)
+        taken(2, p)
+    for bit in range(3):
+        near_arrived(bit, other)
+
+    def multiply(h):
+        start = pl.multiple_of(h * chunk, chunk)
+        return jnp.dot(
+            all_ref[:, pl.ds(start, chunk)], cols_ref[pl.ds(start, chunk), :],
+            preferred_element_type=jnp.float32,
+        )
+
+    hidden_ref[...] = multiply(high)
+
+    def add(s, carry):
+        for h, there in ((high - s, high - s >= 0), (high + s, high + s < highs)):
+            @pl.when(there)
+            def _(h=h):
+                for l in range(SPLIT):
+                    side(h, l, other).wait_recv()
+                hidden_ref[...] += multiply(h)
+
+        return carry
+
+    lax.fori_loop(1, highs, add, 0)
+
+    for bit in range(3):
+        near(bit, 0).wait_send()
+        near(bit, 1).wait_send()
+    for p in range(PIECES):
+        give(0, p).wait_send()
+        give(1, p).wait_send()
+        pass_on(p).wait_send()
+
+    def sent(h, carry):
+        for l in range(SPLIT):
+            pl.when((h <= high) & (high < highs - 1))(lambda: line(True, h, l).wait_send())
+            pl.when((h >= high) & (high > 0))(lambda: line(False, h, l).wait_send())
+            pl.when(h != high)(lambda: side(h, l, part).wait_send())
+        return carry
+
+    lax.fori_loop(0, highs, sent, 0)
+
+
+def pool(coarse, weight):
+    rows, features = coarse.shape
+    width = weight.shape[1] // SPLIT
+    highs = lax.axis_size("tm") // SPLIT
+    dma = pltpu.SemaphoreType.DMA
+    vmem = pl.BlockSpec(memory_space=pltpu.VMEM)
+    return pl.pallas_call(
+        functools.partial(pool_kernel, highs),
+        out_shape=jax.ShapeDtypeStruct((rows * SPLIT, width), jnp.float32),
+        in_specs=[vmem, vmem],
+        out_specs=vmem,
+        scratch_shapes=[
+            pltpu.VMEM((rows * SPLIT, features), jnp.bfloat16),
+            pltpu.VMEM((features, width), jnp.bfloat16),
+            [
+                dma((3, 2)), dma((3, 2)), dma((2,)), dma((2, highs, SPLIT)), dma((highs, SPLIT)),
+                dma((highs, SPLIT)), dma((highs, SPLIT)), dma((3, PIECES)), dma((3, PIECES)),
+            ],
+        ],
+        compiler_params=pltpu.CompilerParams(collective_id=0, has_side_effects=True),
+    )(coarse, weight)
 
 
 def by_lanes(rows):
@@ -168,12 +386,7 @@
     low_groups = [[h * SPLIT + i for i in range(SPLIT)] for h in range(count // SPLIT)]
     high_groups = [[h * SPLIT + i for h in range(count // SPLIT)] for i in range(SPLIT)]
     coarse = signal.reshape(fine_rows // POOL, POOL * channels)
-    coarse = lax.all_gather(coarse, "tm", axis_index_groups=low_groups, axis=0, tiled=True)
-    weight = lax.all_to_all(
-        pool_weight, "tm", 1, 0, axis_index_groups=low_groups, tiled=True
-    )
-    weight = lax.all_gather(weight, "tm", axis_index_groups=high_groups, axis=0, tiled=True)
-    hidden = jnp.dot(coarse, weight, preferred_element_type=jnp.float32)
+    hidden = pool(coarse, pool_weight)
     rows, chans = hidden.shape
 
     def own(array):

time: 239 us -> 153 us (0.64)
  waiting for transfers between devices: 93.9 us -> 0 us
  Pallas kernels: 27.8 us -> 77.5 us
  blocking collectives: 76.9 us -> 54.8 us
  between operations: 13.6 us -> 0.17 us
  matrix products: 5.85 us -> 0 us
  local copies, waits for them, and re-layouts: 7.52 us -> 3.3 us
  other arithmetic: 12.7 us -> 16.1 us
    all_gather x2 -> x0, waiting for transfers between devices: 93.9 us -> none  [the longest x1 82.7 us: local(): lax.all_gather(weight, 'tm', axis_index_groups=high_groups, axis=0, tiled...]
    pallas_call x0 -> x1, Pallas kernels: none -> 49.7 us  [pool(): pl.pallas_call(functools.partial(pool_kernel, highs), out_shape=jax.Shape...]
    all_to_all x1 -> x0, blocking collectives: 25.8 us -> none  [local(): lax.all_to_all(pool_weight, 'tm', 1, 0, axis_index_groups=low_groups, til...]
    dot_general x1 -> x0, matrix products: 5.85 us -> none  [local(): hidden = jnp.dot(coarse, weight, preferred_element_type=jnp.float32)]
    all_gather x2, blocking collectives: 10.4 us -> 15.2 us  [state_layer(): lax.all_gather(jnp.stack([mean, spread]), 'tm', axis_index_groups=low_gro...]
  transfers between devices with their start and end apart: 2 -> 0, of which waited for: 2 -> 0; matrix products, arithmetic and copies ran while one was open for 3% -> 0% of each run, Pallas kernels for 0% -> 0%
where the time goes in v2:
time: 153 us; the launch traced here: 152 us
  Pallas kernels  77.5 us (51%)
  blocking collectives  54.8 us (36%)
  other arithmetic  16.1 us (11%)
  local copies, waits for them, and re-layouts  3.3 us (2%)
    pallas_call x1, Pallas kernels, pool(): pl.pallas_call(functools.partial(pool_kernel, highs), out_shape=jax.Shape...  49.7 us
    all_gather x2, blocking collectives, state_layer(): every = lax.all_gather(last, 'tm', axis_index_groups=high_groups)  28.2 us
    pallas_call x2, Pallas kernels, state_layer(): pl.pallas_call(functools.partial(respond_kernel, modes), grid=grid, in_sp...  17.3 us
    all_gather x2, blocking collectives, state_layer(): lax.all_gather(jnp.stack([mean, spread]), 'tm', axis_index_groups=low_gro...  15.2 us
    all_to_all x1, blocking collectives, local(): lax.all_to_all(hidden.astype(jnp.bfloat16), 'tm', 0, 1, axis_index_groups...  11.5 us
    pallas_call x2, Pallas kernels, state_layer(): pl.pallas_call(functools.partial(ends_kernel, modes), grid=grid, in_specs...  10.5 us

profile of v2, /device:TPU:0, one launch (start us, length us, event | category | flops | bytes accessed | tf_op | source)
XLA Modules:
  0.0 151.9 jit_solution(16261077910082510843)
XLA Ops:
  0.0 0.0 copy-start.2
  0.0 0.9 fusion.11
  0.9 1.0 multiply_bitcast_fusion.1
  1.9 1.8 %bitcast_multiply_fusion = (f32[32,512]{1,0:T(8,128)}, f32[32,512]{1,0:T(8,128)}, f32[32,512]{1,0:T(8,128)}, f32[32,512]{1,0:T(8,128)}, f32[32,512]{1,0:T(8,128)...) fusion(f32[2,32,2048]{2,1,0:T(8,128)} %param.14, s32[]{:T(128)S(6)} %add.111, s32[]{:T(128)S(6)} %select_n.51, ...), kind=kLoop, calls=%fused_computation.18 | loop fusion | flops 196608 | bytes 659592 | tf_op jit(solution)/shard_map/mul | solution.py:326
  3.7 0.7 multiply_exponential_fusion.2
  4.4 0.5 multiply_reduce_fusion
  4.9 0.9 dynamic-slice_add_fusion
  5.8 0.0 copy-start.4
  5.8 0.1 scatter-add.6.kernel_ref
  5.9 0.0 copy-done.2
  5.9 0.0 copy-start.3
  5.9 1.5 reshape.294.coarse_ref
  7.4 49.7 %shard_map.64.hidden_ref = f32[512,512]{1,0:T(8,128)} custom-call(bf16[128,4096]{1,0:T(8,128)(2,1)} %reshape.294.coarse_ref, bf16[256,2048]{1,0:T(8,128)(2,1)} %weight_ref.1), custom_call_target="tpu_custom_call" | custom-call | tf_op jit(solution)/shard_map/pallas_call | solution.py:301
  57.2 0.0 copy-done.4
  57.2 0.0 copy-done.3
  57.2 0.0 copy-start
  57.2 1.5 reduce_sum.108
  58.7 1.5 multiply_reduce_fusion.3
  60.1 10.0 %all-gather.4 = f32[4,2,512]{2,1,0:T(2,128)S(1)} all-gather(f32[1,2,512]{2,1,0:T(2,128)S(1)} %maximum_bitcast_fusion), channel_id=2, replica_groups={{0,1,2,3},{4,5,6,7},{8,9,10,11},{12,13,14,15},{16,17,18,19},{20,21,22,2..., dimensions={0}, use_global_device_ids=true | all-gather | bytes 20480 | tf_op jit(solution)/shard_map/all_gather | solution.py:347
  70.2 0.0 copy-done
  70.2 1.2 multiply_multiply_fusion.1.x_ref
  71.4 5.2 %shard_map.65 = (f32[1024,512]{1,0:T(8,128)}, f32[32,512]{1,0:T(8,128)}) custom-call(f32[512,512]{1,0:T(8,128)} %multiply_multiply_fusion.1.x_ref, f32[32,512]{1,0:T(8,128)} %get-tuple-element.56.decay_ref, f32[32,512]{1,0:T(8,128)} %get-tuple-element.55.step_ref), custom_call_target="tpu_custom_call" | custom-call | tf_op jit(solution)/shard_map/pallas_call | solution.py:354
  76.7 14.1 %all-gather.1 = f32[128,512]{1,0:T(8,128)S(1)} all-gather(f32[32,512]{1,0:T(8,128)} %get-tuple-element.34), channel_id=3, replica_groups={{0,4,8,12},{1,5,9,13},{2,6,10,14},{3,7,11,15},{16,20,24,28},{17,21,25,2..., dimensions={0}, use_global_device_ids=true | all-gather | bytes 327680 | tf_op jit(solution)/shard_map/all_gather | solution.py:364
  90.7 0.7 fusion.3.start_ref
  91.5 8.6 %shard_map.66.hidden_ref = f32[512,512]{1,0:T(8,128)} custom-call(f32[512,512]{1,0:T(8,128)} %multiply_multiply_fusion.1.x_ref, f32[512,512]{1,0:T(8,128)} %shard_map.64.hidden_ref, f32[1024,512]{1,0:T(8,128)} %get-tuple-element.33.ends_in_ref, f32[32,512]{1,0:T(8,128)} %fusion.3.start_ref, f32[32,512]{1,0:T(8,128)} %get-tuple-element.55.step_ref, ...), custom_call_target="tpu_custom_call" | custom-call | tf_op jit(solution)/shard_map/pallas_call | solution.py:369
  100.1 0.0 copy-start.1
  100.1 1.5 reduce_sum.114
  101.6 1.5 multiply_reduce_fusion.1
  103.1 5.2 %all-gather.5 = f32[4,2,512]{2,1,0:T(2,128)S(1)} all-gather(f32[1,2,512]{2,1,0:T(2,128)S(1)} %maximum_bitcast_fusion.1), channel_id=4, replica_groups={{0,1,2,3},{4,5,6,7},{8,9,10,11},{12,13,14,15},{16,17,18,19},{20,21,22,2..., dimensions={0}, use_global_device_ids=true | all-gather | bytes 20480 | tf_op jit(solution)/shard_map/all_gather | solution.py:347
  108.4 0.0 copy-done.1
  108.4 1.2 multiply_multiply_fusion.x_ref
  109.6 5.2 %shard_map.67 = (f32[1024,512]{1,0:T(8,128)}, f32[32,512]{1,0:T(8,128)}) custom-call(f32[512,512]{1,0:T(8,128)} %multiply_multiply_fusion.x_ref, f32[32,512]{1,0:T(8,128)} %get-tuple-element.59.decay_ref, f32[32,512]{1,0:T(8,128)} %get-tuple-element.58.step_ref), custom_call_target="tpu_custom_call" | custom-call | tf_op jit(solution)/shard_map/pallas_call | solution.py:354
  114.8 14.1 %all-gather.3 = f32[128,512]{1,0:T(8,128)S(1)} all-gather(f32[32,512]{1,0:T(8,128)} %get-tuple-element.36), channel_id=5, replica_groups={{0,4,8,12},{1,5,9,13},{2,6,10,14},{3,7,11,15},{16,20,24,28},{17,21,25,2..., dimensions={0}, use_global_device_ids=true | all-gather | bytes 327680 | tf_op jit(solution)/shard_map/all_gather | solution.py:364
  128.9 0.7 fusion.start_ref
  129.6 8.7 %shard_map.68 = f32[512,512]{1,0:T(8,128)} custom-call(f32[512,512]{1,0:T(8,128)} %multiply_multiply_fusion.x_ref, f32[512,512]{1,0:T(8,128)} %shard_map.66.hidden_ref, f32[1024,512]{1,0:T(8,128)} %get-tuple-element.35.ends_in_ref, f32[32,512]{1,0:T(8,128)} %fusion.start_ref, f32[32,512]{1,0:T(8,128)} %get-tuple-element.58.step_ref, ...), custom_call_target="tpu_custom_call" | custom-call | tf_op jit(solution)/shard_map/pallas_call | solution.py:369
  138.3 1.3 convert_element_type.3
  139.6 11.5 %all_to_all.19 = bf16[4,128,512]{2,1,0:T(8,128)(2,1)S(1)} all-to-all(bf16[4,128,512]{2,1,0:T(8,128)(2,1)S(1)} %bitcast.36), channel_id=1, replica_groups={{0,1,2,3},{4,5,6,7},{8,9,10,11},{12,13,14,15},{16,17,18,19},{20,21,22,2..., dimensions={0} | all-to-all | bytes 1048576 | tf_op jit(solution)/shard_map/all_to_all | solution.py:399
  151.0 0.8 copy.12
  (16 shorter events, 0.2 us)
Async XLA Ops:
  0.0 5.9 %copy-start.2 = (bf16[512,1024]{1,0:T(8,128)(2,1)S(1)}, bf16[512,1024]{1,0:T(8,128)(2,1)}, u32[]{:S(2)}) copy-start(bf16[512,1024]{1,0:T(8,128)(2,1)} %param.10) | copy-start | bytes 3145732
  5.8 51.3 %copy-start.4 = (f32[16,512]{1,0:T(8,128)}, f32[16,512]{1,0:T(8,128)S(1)}, u32[]{:S(2)}) copy-start(f32[16,512]{1,0:T(8,128)S(1)} %scatter-add.9.kernel_ref) | copy-start | bytes 98308
  5.9 51.2 %copy-start.3 = (f32[16,512]{1,0:T(8,128)}, f32[16,512]{1,0:T(8,128)S(1)}, u32[]{:S(2)}) copy-start(f32[16,512]{1,0:T(8,128)S(1)} %scatter-add.6.kernel_ref) | copy-start | bytes 98308
  57.2 13.0 %copy-start = (f32[512,512]{1,0:T(8,128)S(1)}, f32[512,512]{1,0:T(8,128)}, u32[]{:S(2)}) copy-start(f32[512,512]{1,0:T(8,128)} %shard_map.64.hidden_ref) | copy-start | bytes 3145732
  100.1 8.2 %copy-start.1 = (f32[512,512]{1,0:T(8,128)S(1)}, f32[512,512]{1,0:T(8,128)}, u32[]{:S(2)}) copy-start(f32[512,512]{1,0:T(8,128)} %shard_map.66.hidden_ref) | copy-start | bytes 3145732

commit v3 on v2

--- a/solution.py
+++ b/solution.py
@@ -78,26 +78,6 @@
     lax.fori_loop(0, rows // span, group, 0)
 
 
-def ends_kernel(modes, x_ref, decay_ref, step_ref, ends_ref, last_ref):
-    cols = slice(None)
-    block_ends(x_ref, decay_ref, ends_ref, modes, cols)
-    zero = [jnp.zeros((8, LANES), jnp.float32)] * (modes // 8)
-    last = scan_blocks(ends_ref, step_ref, modes, cols, zero)
-    for i in range(modes // 8):
-        last_ref[pl.ds(i * 8, 8), cols] = last[i]
-
-
-def respond_kernel(
-    modes, x_ref, hidden_ref, ends_in_ref, start_ref, step_ref, out_ref, powers_ref, kernel_ref,
-    result_ref, ends_ref
-):
-    cols = slice(None)
-    ends_ref[...] = ends_in_ref[...]
-    start = [start_ref[pl.ds(i * 8, 8), cols] for i in range(modes // 8)]
-    scan_blocks(ends_ref, step_ref, modes, cols, start, out_ref)
-    respond(x_ref, hidden_ref, ends_ref, powers_ref, kernel_ref, result_ref, modes, cols)
-
-
 MESH = pl.DeviceIdType.MESH
 
 
@@ -260,7 +240,12 @@
             preferred_element_type=jnp.float32,
         )
 
-    hidden_ref[...] = multiply(high)
+    def keep(value, first):
+        for g in range(width // LANES):
+            piece_of = value[:, g * LANES : (g + 1) * LANES]
+            hidden_ref[g] = piece_of if first else hidden_ref[g] + piece_of
+
+    keep(multiply(high), True)
 
     def add(s, carry):
         for h, there in ((high - s, high - s >= 0), (high + s, high + s < highs)):
@@ -268,7 +253,7 @@
             def _(h=h):
                 for l in range(SPLIT):
                     side(h, l, other).wait_recv()
-                hidden_ref[...] += multiply(h)
+                keep(multiply(h), False)
 
         return carry
 
@@ -300,7 +285,7 @@
     vmem = pl.BlockSpec(memory_space=pltpu.VMEM)
     return pl.pallas_call(
         functools.partial(pool_kernel, highs),
-        out_shape=jax.ShapeDtypeStruct((rows * SPLIT, width), jnp.float32),
+        out_shape=jax.ShapeDtypeStruct((width // LANES, rows * SPLIT, LANES), jnp.float32),
         in_specs=[vmem, vmem],
         out_specs=vmem,
         scratch_shapes=[
@@ -315,10 +300,6 @@
     )(coarse, weight)
 
 
-def by_lanes(rows):
-    return pl.BlockSpec((rows, LANES), lambda i: (0, i))
-
-
 def tables(step_row, out_mix, skip_row, rows):
     modes = out_mix.shape[0]
     rates = step_row[None, :] * (jnp.arange(modes, dtype=jnp.float32) + 1.0)[:, None]
@@ -328,77 +309,217 @@
     kernel = jnp.sum(out[None] * jnp.exp(-lags[:, None, None] * rates[None]), axis=1)
     kernel = kernel.at[0].add(skip_row)
     powers = jnp.exp(-(lags + 1.0)[:, None] * step_row[None, :])
-    return {
-        "decay": jnp.exp(-rates),
-        "step": jnp.exp(-rates * BLOCK),
-        "whole": jnp.exp(-rates * rows),
-        "out": out,
-        "powers": powers,
-        "kernel": kernel,
-    }
-
-
-def state_layer(hidden, gain, table, low_groups, high_groups):
-    rows, chans = hidden.shape
-    modes = table["decay"].shape[0]
-    blocks = rows // BLOCK
-    mean = jnp.mean(hidden, axis=-1)
-    spread = jnp.sum(jnp.square(hidden - mean[:, None]), axis=-1)
-    stats = lax.all_gather(jnp.stack([mean, spread]), "tm", axis_index_groups=low_groups)
-    row_mean = jnp.mean(stats[:, 0], axis=0)
-    row_var = (
-        jnp.sum(stats[:, 1], axis=0) + chans * jnp.sum(jnp.square(stats[:, 0] - row_mean), axis=0)
-    ) / (chans * SPLIT)
-    normed = (hidden - row_mean[:, None]) * lax.rsqrt(row_var + 1e-05)[:, None] * gain[None, :]
-    grid = (chans // LANES,)
-    ends, last = pl.pallas_call(
-        functools.partial(ends_kernel, modes),
-        grid=grid,
-        in_specs=[by_lanes(rows), by_lanes(modes), by_lanes(modes)],
-        out_specs=[by_lanes(modes * blocks), by_lanes(modes)],
-        out_shape=[
-            jax.ShapeDtypeStruct((modes * blocks, chans), jnp.float32),
-            jax.ShapeDtypeStruct((modes, chans), jnp.float32),
+    return jnp.concatenate(
+        [jnp.exp(-rates), jnp.exp(-rates * BLOCK), jnp.exp(-rates * rows), out]
+        + [jnp.pad(extra, ((0, modes - BLOCK), (0, 0))) for extra in (powers, kernel)]
+    )
+
+
+def layers_kernel(
+    highs, modes, hidden_in_ref, gain_ref, table_ref, out_ref, hidden_ref, x_ref, ends_ref,
+    stats_ref, last_ref, states_ref, rounded_ref, sems
+):
+    stats_send, stats_recv, state_send, state_recv, out_send, out_recv = sems
+    part, place = lax.axis_index("parts"), lax.axis_index("tm")
+    high, low = place // SPLIT, place % SPLIT
+    groups, rows, _ = hidden_in_ref.shape
+    chans = groups * LANES
+    layers = gain_ref.shape[0]
+    flip = lambda bit: low + bit - 2 * bit * ((low // bit) % 2)
+    near = (flip(1), flip(2), SPLIT - 1 - low)
+    at = lambda h, l: (part, h * SPLIT + l)
+    own_rows = rows // SPLIT
+    exact = lax.Precision.HIGHEST
+
+    barrier = pltpu.get_barrier_semaphore()
+
+    def greet(device):
+        pl.semaphore_signal(barrier, inc=1, device_id=device, device_id_type=MESH)
+
+    for who in near:
+        greet(at(high, who))
+
+    def greet_high(h, carry):
+        pl.when(h != high)(lambda: greet(at(h, low)))
+        return carry
+
+    lax.fori_loop(0, highs, greet_high, 0)
+
+    def stats_copy(l, bit, owner):
+        return pltpu.make_async_remote_copy(
+            stats_ref.at[l, owner], stats_ref.at[l, owner], stats_send.at[l, bit],
+            stats_recv.at[l, bit], device_id=at(high, near[bit]), device_id_type=MESH,
+        )
+
+    def state_copy(l, g, source, target):
+        return pltpu.make_async_remote_copy(
+            last_ref.at[l, g], states_ref.at[l, source, g], state_send.at[l, target, g],
+            state_recv.at[l, source, g], device_id=at(target, low), device_id_type=MESH,
+        )
+
+    def out_cols(owner, g):
+        return pl.ds(pl.multiple_of(owner * chans + g * LANES, LANES), LANES)
+
+    def out_copy(g, bit, owner):
+        start = pl.multiple_of(near[bit] * own_rows, own_rows)
+        return pltpu.make_async_remote_copy(
+            rounded_ref.at[g, pl.ds(start, own_rows), :], out_ref.at[:, out_cols(owner, g)],
+            out_send.at[g, bit], out_recv.at[g, bit],
+            device_id=at(high, near[bit]), device_id_type=MESH,
+        )
+
+    for l in range(layers):
+        source_ref = hidden_in_ref if l == 0 else hidden_ref
+        total = source_ref[0]
+        for g in range(1, groups):
+            total = total + source_ref[g]
+        mean = jnp.sum(total, axis=-1, keepdims=True) / chans
+        square = jnp.square(source_ref[0] - mean)
+        for g in range(1, groups):
+            square = square + jnp.square(source_ref[g] - mean)
+        ones = jnp.ones((8, LANES), jnp.float32)
+        across = lambda v: lax.dot_general(
+            ones, v, (((1,), (1,)), ((), ())), precision=exact, preferred_element_type=jnp.float32
+        )
+        line = lax.broadcasted_iota(jnp.int32, (8, rows), 0)
+        stats_ref[l, low] = jnp.where(line == 0, across(total) / chans, across(square))
+        if l == 0:
+            pl.semaphore_wait(barrier, 3 + highs - 1)
+        for bit in (1, 2, 0):
+            stats_copy(l, bit, low).start()
+        for bit in range(3):
+            stats_copy(l, bit, near[bit]).wait_recv()
+        every = [stats_ref[l, i] for i in range(SPLIT)]
+        means = [e[0:1] for e in every]
+        row_mean = (means[0] + means[1] + means[2] + means[3]) / SPLIT
+        row_var = sum(e[1:2] + chans * jnp.square(e[0:1] - row_mean) for e in every)
+        row_scale = lax.rsqrt(row_var / (chans * SPLIT) + 1e-05)
+        both = jnp.where(line == 0, row_mean, row_scale)
+        both = jnp.transpose(both)
+        row_mean, row_scale = both[:, 0:1], both[:, 1:2]
+        for g in range(groups):
+            gain = gain_ref[pl.ds(l, 1), pl.ds(g * LANES, LANES)]
+            x_ref[g] = (source_ref[g] - row_mean) * row_scale * gain
+
+        def table(index, g, size):
+            return table_ref.at[l, pl.ds(index * modes, size), pl.ds(pl.multiple_of(g * LANES, LANES), LANES)]
+
+        cols = slice(None)
+        eights = modes // 8
+
+        def send(g):
+            def one(h, carry):
+                pl.when(h > high)(lambda: state_copy(l, g, high, h).start())
+                return carry
+
+            lax.fori_loop(1, highs, one, 0)
+
+        def ends(g, carry):
+            block_ends(x_ref.at[g], table(0, g, modes), ends_ref.at[g], modes, cols)
+            zero = [jnp.zeros((8, LANES), jnp.float32)] * eights
+            last = scan_blocks(ends_ref.at[g], table(1, g, modes), modes, cols, zero)
+            for i in range(eights):
+                last_ref[l, g, pl.ds(i * 8, 8), :] = last[i]
+            send(g)
+            return carry
+
+        lax.fori_loop(0, groups, ends, 0)
+
+        def finish(g, carry):
+            whole = table(2, g, modes)
+
+            def join(h, start):
+                @pl.when(h < high)
+                def _():
+                    state_copy(l, g, h, high).wait_recv()
+                    states_ref[l, high, g] = whole[...] * states_ref[l, high, g] + states_ref[l, h, g]
+                return start
+
+            states_ref[l, high, g] = jnp.zeros((modes, LANES), jnp.float32)
+            lax.fori_loop(0, highs - 1, join, 0)
+            start = [states_ref[l, high, g, pl.ds(i * 8, 8), :] for i in range(eights)]
+            scan_blocks(
+                ends_ref.at[g], table(1, g, modes), modes, cols, start, table(3, g, modes)
+            )
+            respond(
+                x_ref.at[g], source_ref.at[g], ends_ref.at[g], table(4, g, BLOCK),
+                table(5, g, BLOCK), hidden_ref.at[g], modes, cols,
+            )
+            if l == layers - 1:
+                rounded_ref[g] = hidden_ref[g].astype(jnp.bfloat16)
+                for bit in (1, 2, 0):
+                    out_copy(g, bit, low).start()
+                out_ref[:, out_cols(low, g)] = rounded_ref[
+                    g, pl.ds(pl.multiple_of(low * own_rows, own_rows), own_rows), :
+                ]
+            return carry
+
+        lax.fori_loop(0, groups, finish, 0)
+
+    def drain(g, carry):
+        for bit in range(3):
+            out_copy(g, bit, near[bit]).wait_recv()
+            out_copy(g, bit, low).wait_send()
+
+        def one(h, carry):
+            @pl.when(h > high)
+            def _():
+                for l in range(layers):
+                    state_copy(l, g, high, h).wait_send()
+            return carry
+
+        return lax.fori_loop(1, highs, one, carry)
+
+    lax.fori_loop(0, groups, drain, 0)
+    for l in range(layers):
+        for bit in range(3):
+            stats_copy(l, bit, low).wait_send()
+
+
+def run_layers(hidden, gain, table, modes):
+    groups, rows, _ = hidden.shape
+    layers = gain.shape[0]
+    highs = lax.axis_size("tm") // SPLIT
+    dma = pltpu.SemaphoreType.DMA
+    vmem = pl.BlockSpec(memory_space=pltpu.VMEM)
+    f32 = jnp.float32
+    return pl.pallas_call(
+        functools.partial(layers_kernel, highs, modes),
+        out_shape=jax.ShapeDtypeStruct((rows // SPLIT, groups * LANES * SPLIT), jnp.bfloat16),
+        in_specs=[vmem] * 3,
+        out_specs=vmem,
+        scratch_shapes=[
+            pltpu.VMEM((groups, rows, LANES), f32),
+            pltpu.VMEM((groups, rows, LANES), f32),
+            pltpu.VMEM((groups, modes * (rows // BLOCK), LANES), f32),
+            pltpu.VMEM((layers, SPLIT, 8, rows), f32),
+            pltpu.VMEM((layers, groups, modes, LANES), f32),
+            pltpu.VMEM((layers, highs, groups, modes, LANES), f32),
+            pltpu.VMEM((groups, rows, LANES), jnp.bfloat16),
+            [
+                dma((layers, 3)), dma((layers, 3)), dma((layers, highs, groups)),
+                dma((layers, highs, groups)), dma((groups, 3)), dma((groups, 3)),
+            ],
         ],
-    )(normed, table["decay"], table["step"])
-    every = lax.all_gather(last, "tm", axis_index_groups=high_groups)
-    mine = lax.axis_index("tm") // SPLIT
-    start = jnp.zeros_like(last)
-    for p in range(len(high_groups[0]) - 1):
-        start = jnp.where(p < mine, table["whole"] * start + every[p], start)
-    return pl.pallas_call(
-        functools.partial(respond_kernel, modes),
-        grid=grid,
-        in_specs=[
-            by_lanes(rows), by_lanes(rows), by_lanes(modes * blocks), by_lanes(modes),
-            by_lanes(modes), by_lanes(modes), by_lanes(BLOCK), by_lanes(BLOCK),
-        ],
-        out_specs=by_lanes(rows),
-        out_shape=jax.ShapeDtypeStruct((rows, chans), jnp.float32),
-        scratch_shapes=[pltpu.VMEM((modes * blocks, LANES), jnp.float32)],
-    )(normed, hidden, ends, start, table["step"], table["out"], table["powers"], table["kernel"])
+        compiler_params=pltpu.CompilerParams(collective_id=1, has_side_effects=True),
+    )(hidden, gain, table)
 
 
 def local(signal, pool_weight, norm_gain, step_size, mode_out, skip_gain):
     fine_rows, channels = signal.shape
-    count = lax.axis_size("tm")
     low = lax.axis_index("tm") % SPLIT
-    low_groups = [[h * SPLIT + i for i in range(SPLIT)] for h in range(count // SPLIT)]
-    high_groups = [[h * SPLIT + i for h in range(count // SPLIT)] for i in range(SPLIT)]
     coarse = signal.reshape(fine_rows // POOL, POOL * channels)
-    hidden = pool(coarse, pool_weight)
-    rows, chans = hidden.shape
+    chans = pool_weight.shape[1] // SPLIT
+    rows = SPLIT * coarse.shape[0]
+    modes = mode_out.shape[1]
 
     def own(array):
         return lax.dynamic_slice_in_dim(array, low * chans, chans, axis=array.ndim - 1)
 
     gain, step, mix, skip = own(norm_gain), own(step_size), own(mode_out), own(skip_gain)
-    for l in range(norm_gain.shape[0]):
-        table = tables(step[l], mix[l], skip[l], rows)
-        hidden = state_layer(hidden, gain[l], table, low_groups, high_groups)
-    return lax.all_to_all(
-        hidden.astype(jnp.bfloat16), "tm", 0, 1, axis_index_groups=low_groups, tiled=True
-    )
+    table = jax.vmap(functools.partial(tables, rows=rows))(step, mix, skip)
+    hidden = pool(coarse, pool_weight)
+    return run_layers(hidden, gain, table, modes)
 
 
 def solution(mesh):

time: 153 us -> 99.1 us (0.65)
  blocking collectives: 54.8 us -> 0 us
  other arithmetic: 16.1 us -> 2.08 us
  Pallas kernels: 77.5 us -> 91.2 us
  local copies, waits for them, and re-layouts: 3.3 us -> 5.42 us
    all_gather x4 -> x0, blocking collectives: 43.4 us -> none  [the longest x2 28.2 us: state_layer(): every = lax.all_gather(last, 'tm', axis_index_groups=high_groups)]
    pallas_call x4 -> x1, Pallas kernels: 27.8 us -> 41.4 us  [run_layers(): pl.pallas_call(functools.partial(layers_kernel, highs, modes), out_shape=...]
    all_to_all x1 -> x0, blocking collectives: 11.5 us -> none  [local(): lax.all_to_all(hidden.astype(jnp.bfloat16), 'tm', 0, 1, axis_index_groups...]
    reduce_sum x8 -> x0, other arithmetic: 5.97 us -> none  [the longest x2 2.95 us: state_layer(): spread = jnp.sum(jnp.square(hidden - mean[:, None]), axis=-1)]
    mul x4 -> x1, other arithmetic: 5.17 us -> 0.1 us  [tables(): step_row[None, :] * (jnp.arange(modes, dtype=jnp.float32) + 1.0)[:, None]]
    unnamed x10 -> x8, local copies, waits for them, and re-layouts: 0.02 us -> 2.59 us
where the time goes in v3:
time: 99.1 us; the launch traced here: 98.8 us
  Pallas kernels  91.2 us (92%)
  local copies, waits for them, and re-layouts  5.42 us (5%)
  other arithmetic  2.08 us (2%)
    pallas_call x1, Pallas kernels, pool(): pl.pallas_call(functools.partial(pool_kernel, highs), out_shape=jax.Shape...  49.7 us
    pallas_call x1, Pallas kernels, run_layers(): pl.pallas_call(functools.partial(layers_kernel, highs, modes), out_shape=...  41.4 us
    unnamed x8, local copies, waits for them, and re-layouts  2.59 us

profile of v3, /device:TPU:0, one launch (start us, length us, event | category | flops | bytes accessed | tf_op | source)
XLA Modules:
  0.0 98.8 jit_solution(2001288694450629992)
XLA Ops:
  0.0 0.0 copy-start
  0.0 0.7 copy-done
  0.7 0.6 constant_dynamic-slice_fusion.2.gain_ref
  1.3 0.7 constant_dynamic-slice_fusion
  2.0 0.1 multiply_exponential_fusion
  2.1 0.1 exponential_dynamic-update-slice_fusion.2
  2.2 0.0 copy-start.2
  2.2 0.1 broadcast_multiply_fusion
  2.3 0.1 exponential_dynamic-update-slice_fusion
  2.4 1.2 %constant_dynamic-update-slice_fusion = (f32[2,192,512]{2,1,0:T(8,128)S(1)}, f32[2,32,512]{2,1,0:T(8,128)S(1)}) fusion(f32[2,192,512]{2,1,0:T(8,128)S(1)} %exponential_dynamic-update-slice_fusion, f32[32]{0:T(128)S(1)} %iota_add_fusion, f32[2,512]{1,0:T(2,128)S(1)} %get-tuple-element.22, f32[2,32,2048]{2,1,0:T(8,128)} %param.12, s32[]{:T(128)S(6)} %select_n.14), kind=kLoop, calls=%fused_computation.9 | loop fusion | flops 131072 | bytes 397828
  3.6 0.5 multiply_reduce_fusion
  4.1 0.1 scatter-add.4
  4.2 0.0 copy-done.2
  4.2 0.0 copy-start.1
  4.3 1.4 %reshape.56.coarse_ref = bf16[128,4096]{1,0:T(8,128)(2,1)} reshape(bf16[512,1024]{1,0:T(8,128)(2,1)S(1)} %copy-done.2) | data formatting | bytes 2097152 | tf_op jit(solution)/shard_map/reshape | solution.py:511
  5.7 49.7 %shard_map.64.hidden_in_ref = f32[4,512,128]{2,1,0:T(8,128)} custom-call(bf16[128,4096]{1,0:T(8,128)(2,1)} %reshape.56.coarse_ref, bf16[256,2048]{1,0:T(8,128)(2,1)} %weight_ref.1), custom_call_target="tpu_custom_call" | custom-call | tf_op jit(solution)/shard_map/pallas_call | solution.py:286
  55.4 0.0 copy-done.1
  55.4 41.4 %shard_map.65 = bf16[128,2048]{1,0:T(8,128)(2,1)} custom-call(f32[4,512,128]{2,1,0:T(8,128)} %shard_map.64.hidden_in_ref, f32[2,512]{1,0:T(2,128)} %constant_dynamic-slice_fusion.2.gain_ref, f32[2,192,512]{2,1,0:T(8,128)} %copy-done.1), custom_call_target="tpu_custom_call" | custom-call | tf_op jit(solution)/shard_map/pallas_call | solution.py:486
  96.9 1.9 %copy.14 = bf16[128,2048]{1,0:T(8,128)(2,1)} copy(bf16[128,2048]{1,0:T(8,128)(2,1)} %shard_map.65) | data formatting | bytes 1048576
  (6 shorter events, 0.1 us)
Async XLA Ops:
  0.0 0.7 copy-start
  2.2 2.0 %copy-start.2 = (bf16[512,1024]{1,0:T(8,128)(2,1)S(1)}, bf16[512,1024]{1,0:T(8,128)(2,1)}, u32[]{:S(2)}) copy-start(bf16[512,1024]{1,0:T(8,128)(2,1)} %param.8) | copy-start | bytes 3145732
  4.2 51.2 %copy-start.1 = (f32[2,192,512]{2,1,0:T(8,128)}, f32[2,192,512]{2,1,0:T(8,128)S(1)}, u32[]{:S(2)}) copy-start(f32[2,192,512]{2,1,0:T(8,128)S(1)} %pad_dynamic-update-slice_fusion.table_ref) | copy-start | bytes 2359300

commit v4 on v3

--- a/solution.py
+++ b/solution.py
@@ -12,12 +12,14 @@
 BLOCK = 16
 LANES = 128
 PIECES = 4
+PAD = 8
 
 
 def block_ends(x_ref, decay_ref, ends_ref, modes, cols):
     rows = x_ref.shape[0]
     blocks = rows // BLOCK
     span = 8 * BLOCK
+    pitch = ends_ref.shape[0] // blocks
 
     def group(g, carry):
         base = pl.multiple_of(g * span, span)
@@ -27,21 +29,21 @@
             end = xs[0]
             for j in range(1, BLOCK):
                 end = end * decay + xs[j]
-            ends_ref[pl.ds(pl.multiple_of(n * blocks + g * 8, 8), 8), cols] = end
+            ends_ref[pl.ds(g * 8 * pitch + n, 8, stride=pitch), cols] = end
         return carry
 
     lax.fori_loop(0, rows // span, group, 0)
 
 
-def scan_blocks(ends_ref, step_ref, modes, cols, start, out_ref=None):
-    blocks = ends_ref.shape[0] // modes
+def scan_blocks(blocks, ends_ref, step_ref, modes, cols, start, out_ref=None):
+    pitch = ends_ref.shape[0] // blocks
     groups = modes // 8
     steps = [step_ref[pl.ds(i * 8, 8), cols] for i in range(groups)]
     outs = [out_ref[pl.ds(i * 8, 8), cols] for i in range(groups)] if out_ref is not None else None
     states = list(start)
     for b in range(blocks):
         for i in range(groups):
-            where = pl.ds(i * 8 * blocks + b, 8, stride=blocks)
+            where = pl.ds(b * pitch + i * 8, 8)
             end = ends_ref[where, cols]
             if outs is not None:
                 ends_ref[where, cols] = states[i] * outs[i]
@@ -53,12 +55,11 @@
     rows = x_ref.shape[0]
     blocks = rows // BLOCK
     span = 8 * BLOCK
+    pitch = ends_ref.shape[0] // blocks
 
     def group(g, carry):
         base = pl.multiple_of(g * span, span)
-        coefs = [
-            ends_ref[pl.ds(pl.multiple_of(n * blocks + g * 8, 8), 8), cols] for n in range(modes)
-        ]
+        coefs = [ends_ref[pl.ds(g * 8 * pitch + n, 8, stride=pitch), cols] for n in range(modes)]
         xs = [x_ref[pl.ds(base + j, 8, stride=BLOCK), cols] for j in range(BLOCK)]
         for j in range(BLOCK):
             power = jnp.broadcast_to(powers_ref[pl.ds(j, 1), cols], (8, LANES))
@@ -199,21 +200,24 @@
         near_arrived(bit, part)
         both_ways(high, who)
 
+    def relay(s, l):
+        @pl.when(high - s >= 0)
+        def _():
+            h = high - s
+            line(True, h, l).wait_recv()
+            pl.when(high < highs - 1)(lambda: line(True, h, l).start())
+            side(h, l, part).start()
+
+        @pl.when(high + s < highs)
+        def _():
+            h = high + s
+            line(False, h, l).wait_recv()
+            pl.when(high > 0)(lambda: line(False, h, l).start())
+            side(h, l, part).start()
+
     def step(s, carry):
         for l in range(SPLIT):
-            @pl.when(high - s >= 0)
-            def _():
-                h = high - s
-                line(True, h, l).wait_recv()
-                pl.when(high < highs - 1)(lambda: line(True, h, l).start())
-                side(h, l, part).start()
-
-            @pl.when(high + s < highs)
-            def _():
-                h = high + s
-                line(False, h, l).wait_recv()
-                pl.when(high > 0)(lambda: line(False, h, l).start())
-                side(h, l, part).start()
+            relay(s, l)
 
         @pl.when(s < PIECES)
         def _():
@@ -222,8 +226,11 @@
 
         return carry
 
-    lax.fori_loop(1, highs, step, 0)
-    for p in range(min(PIECES - 1, highs - 1), PIECES):
+    last = highs - 1
+    lax.fori_loop(1, last, step, 0)
+    for l in range(SPLIT - 1):
+        relay(last, l)
+    for p in range(min(PIECES - 1, last - 1), PIECES):
         taken(1, p)
         pass_on(p).start()
     own_rows.wait()
@@ -257,7 +264,9 @@
 
         return carry
 
-    lax.fori_loop(1, highs, add, 0)
+    lax.fori_loop(1, last, add, 0)
+    relay(last, SPLIT - 1)
+    add(last, 0)
 
     for bit in range(3):
         near(bit, 0).wait_send()
@@ -329,6 +338,7 @@
     near = (flip(1), flip(2), SPLIT - 1 - low)
     at = lambda h, l: (part, h * SPLIT + l)
     own_rows = rows // SPLIT
+    blocks = rows // BLOCK
     exact = lax.Precision.HIGHEST
 
     barrier = pltpu.get_barrier_semaphore()
@@ -417,7 +427,7 @@
         def ends(g, carry):
             block_ends(x_ref.at[g], table(0, g, modes), ends_ref.at[g], modes, cols)
             zero = [jnp.zeros((8, LANES), jnp.float32)] * eights
-            last = scan_blocks(ends_ref.at[g], table(1, g, modes), modes, cols, zero)
+            last = scan_blocks(blocks, ends_ref.at[g], table(1, g, modes), modes, cols, zero)
             for i in range(eights):
                 last_ref[l, g, pl.ds(i * 8, 8), :] = last[i]
             send(g)
@@ -439,7 +449,7 @@
             lax.fori_loop(0, highs - 1, join, 0)
             start = [states_ref[l, high, g, pl.ds(i * 8, 8), :] for i in range(eights)]
             scan_blocks(
-                ends_ref.at[g], table(1, g, modes), modes, cols, start, table(3, g, modes)
+                blocks, ends_ref.at[g], table(1, g, modes), modes, cols, start, table(3, g, modes)
             )
             respond(
                 x_ref.at[g], source_ref.at[g], ends_ref.at[g], table(4, g, BLOCK),
@@ -491,7 +501,7 @@
         scratch_shapes=[
             pltpu.VMEM((groups, rows, LANES), f32),
             pltpu.VMEM((groups, rows, LANES), f32),
-            pltpu.VMEM((groups, modes * (rows // BLOCK), LANES), f32),
+            pltpu.VMEM((groups, (modes + PAD) * (rows // BLOCK), LANES), f32),
             pltpu.VMEM((layers, SPLIT, 8, rows), f32),
             pltpu.VMEM((layers, groups, modes, LANES), f32),
             pltpu.VMEM((layers, highs, groups, modes, LANES), f32),

time: 99.1 us -> 94.8 us (0.957)
  Pallas kernels: 91.2 us -> 86.5 us
    pallas_call x1, Pallas kernels: 41.4 us -> 35.9 us  [run_layers(): pl.pallas_call(functools.partial(layers_kernel, highs, modes), out_shape=...]
where the time goes in v4:
time: 94.8 us; the launch traced here: 94.2 us
  Pallas kernels  86.5 us (91%)
  local copies, waits for them, and re-layouts  5.42 us (6%)
  other arithmetic  2.08 us (2%)
    pallas_call x1, Pallas kernels, pool(): pl.pallas_call(functools.partial(pool_kernel, highs), out_shape=jax.Shape...  50.7 us
    pallas_call x1, Pallas kernels, run_layers(): pl.pallas_call(functools.partial(layers_kernel, highs, modes), out_shape=...  35.9 us
    unnamed x8, local copies, waits for them, and re-layouts  2.59 us

profile of v4, /device:TPU:0, one launch (start us, length us, event | category | flops | bytes accessed | tf_op | source)
XLA Modules:
  0.0 94.2 jit_solution(13677579198818662835)
XLA Ops:
  0.0 0.0 copy-start
  0.0 0.7 copy-done
  0.7 0.6 constant_dynamic-slice_fusion.2.gain_ref
  1.3 0.7 constant_dynamic-slice_fusion
  2.0 0.1 multiply_exponential_fusion
  2.1 0.1 exponential_dynamic-update-slice_fusion.2
  2.2 0.0 copy-start.2
  2.2 0.1 broadcast_multiply_fusion
  2.3 0.1 exponential_dynamic-update-slice_fusion
  2.4 1.2 %constant_dynamic-update-slice_fusion = (f32[2,192,512]{2,1,0:T(8,128)S(1)}, f32[2,32,512]{2,1,0:T(8,128)S(1)}) fusion(f32[2,192,512]{2,1,0:T(8,128)S(1)} %exponential_dynamic-update-slice_fusion, f32[32]{0:T(128)S(1)} %iota_add_fusion, f32[2,512]{1,0:T(2,128)S(1)} %get-tuple-element.22, f32[2,32,2048]{2,1,0:T(8,128)} %param.12, s32[]{:T(128)S(6)} %select_n.14), kind=kLoop, calls=%fused_computation.9 | loop fusion | flops 131072 | bytes 397828
  3.6 0.5 multiply_reduce_fusion
  4.1 0.1 scatter-add.4
  4.2 0.0 copy-done.2
  4.2 0.0 copy-start.1
  4.3 1.4 %reshape.56.coarse_ref = bf16[128,4096]{1,0:T(8,128)(2,1)} reshape(bf16[512,1024]{1,0:T(8,128)(2,1)S(1)} %copy-done.2) | data formatting | bytes 2097152 | tf_op jit(solution)/shard_map/reshape | solution.py:521
  5.7 50.7 %shard_map.64.hidden_in_ref = f32[4,512,128]{2,1,0:T(8,128)} custom-call(bf16[128,4096]{1,0:T(8,128)(2,1)} %reshape.56.coarse_ref, bf16[256,2048]{1,0:T(8,128)(2,1)} %weight_ref.1), custom_call_target="tpu_custom_call" | custom-call | tf_op jit(solution)/shard_map/pallas_call | solution.py:295
  56.4 0.0 copy-done.1
  56.4 35.9 %shard_map.65 = bf16[128,2048]{1,0:T(8,128)(2,1)} custom-call(f32[4,512,128]{2,1,0:T(8,128)} %shard_map.64.hidden_in_ref, f32[2,512]{1,0:T(2,128)} %constant_dynamic-slice_fusion.2.gain_ref, f32[2,192,512]{2,1,0:T(8,128)} %copy-done.1), custom_call_target="tpu_custom_call" | custom-call | tf_op jit(solution)/shard_map/pallas_call | solution.py:496
  92.3 1.9 %copy.14 = bf16[128,2048]{1,0:T(8,128)(2,1)} copy(bf16[128,2048]{1,0:T(8,128)(2,1)} %shard_map.65) | data formatting | bytes 1048576
  (6 shorter events, 0.1 us)
Async XLA Ops:
  0.0 0.7 copy-start
  2.2 2.0 %copy-start.2 = (bf16[512,1024]{1,0:T(8,128)(2,1)S(1)}, bf16[512,1024]{1,0:T(8,128)(2,1)}, u32[]{:S(2)}) copy-start(bf16[512,1024]{1,0:T(8,128)(2,1)} %param.8) | copy-start | bytes 3145732
  4.2 52.1 %copy-start.1 = (f32[2,192,512]{2,1,0:T(8,128)}, f32[2,192,512]{2,1,0:T(8,128)S(1)}, u32[]{:S(2)}) copy-start(f32[2,192,512]{2,1,0:T(8,128)S(1)} %pad_dynamic-update-slice_fusion.table_ref) | copy-start | bytes 2359300

commit v5 on v4

--- a/solution.py
+++ b/solution.py
@@ -12,7 +12,7 @@
 BLOCK = 16
 LANES = 128
 PIECES = 4
-PAD = 8
+PAD = 1
 
 
 def block_ends(x_ref, decay_ref, ends_ref, modes, cols):

time: 94.8 us -> 94.7 us (level)
  no operation moved by 1% of the time
where the time goes in v5:
time: 94.7 us; the launch traced here: 93.8 us
  Pallas kernels  86.2 us (91%)
  local copies, waits for them, and re-layouts  5.42 us (6%)
  other arithmetic  2.08 us (2%)
    pallas_call x1, Pallas kernels, pool(): pl.pallas_call(functools.partial(pool_kernel, highs), out_shape=jax.Shape...  50.7 us
    pallas_call x1, Pallas kernels, run_layers(): pl.pallas_call(functools.partial(layers_kernel, highs, modes), out_shape=...  35.6 us
    unnamed x8, local copies, waits for them, and re-layouts  2.59 us

profile of v5, /device:TPU:0, one launch (start us, length us, event | category | flops | bytes accessed | tf_op | source)
XLA Modules:
  0.0 93.8 jit_solution(658891307316446584)
XLA Ops:
  0.0 0.0 copy-start
  0.0 0.7 copy-done
  0.7 0.6 constant_dynamic-slice_fusion.2.gain_ref
  1.3 0.7 constant_dynamic-slice_fusion
  2.0 0.1 multiply_exponential_fusion
  2.1 0.1 exponential_dynamic-update-slice_fusion.2
  2.2 0.0 copy-start.2
  2.2 0.1 broadcast_multiply_fusion
  2.3 0.1 exponential_dynamic-update-slice_fusion
  2.4 1.2 %constant_dynamic-update-slice_fusion = (f32[2,192,512]{2,1,0:T(8,128)S(1)}, f32[2,32,512]{2,1,0:T(8,128)S(1)}) fusion(f32[2,192,512]{2,1,0:T(8,128)S(1)} %exponential_dynamic-update-slice_fusion, f32[32]{0:T(128)S(1)} %iota_add_fusion, f32[2,512]{1,0:T(2,128)S(1)} %get-tuple-element.22, f32[2,32,2048]{2,1,0:T(8,128)} %param.12, s32[]{:T(128)S(6)} %select_n.14), kind=kLoop, calls=%fused_computation.9 | loop fusion | flops 131072 | bytes 397828
  3.6 0.5 multiply_reduce_fusion
  4.1 0.1 scatter-add.4
  4.2 0.0 copy-done.2
  4.2 0.0 copy-start.1
  4.3 1.4 %reshape.56.coarse_ref = bf16[128,4096]{1,0:T(8,128)(2,1)} reshape(bf16[512,1024]{1,0:T(8,128)(2,1)S(1)} %copy-done.2) | data formatting | bytes 2097152 | tf_op jit(solution)/shard_map/reshape | solution.py:521
  5.7 50.7 %shard_map.64.hidden_in_ref = f32[4,512,128]{2,1,0:T(8,128)} custom-call(bf16[128,4096]{1,0:T(8,128)(2,1)} %reshape.56.coarse_ref, bf16[256,2048]{1,0:T(8,128)(2,1)} %weight_ref.1), custom_call_target="tpu_custom_call" | custom-call | tf_op jit(solution)/shard_map/pallas_call | solution.py:295
  56.4 0.0 copy-done.1
  56.4 35.6 %shard_map.65 = bf16[128,2048]{1,0:T(8,128)(2,1)} custom-call(f32[4,512,128]{2,1,0:T(8,128)} %shard_map.64.hidden_in_ref, f32[2,512]{1,0:T(2,128)} %constant_dynamic-slice_fusion.2.gain_ref, f32[2,192,512]{2,1,0:T(8,128)} %copy-done.1), custom_call_target="tpu_custom_call" | custom-call | tf_op jit(solution)/shard_map/pallas_call | solution.py:496
  91.9 1.9 %copy.14 = bf16[128,2048]{1,0:T(8,128)(2,1)} copy(bf16[128,2048]{1,0:T(8,128)(2,1)} %shard_map.65) | data formatting | bytes 1048576
  (6 shorter events, 0.1 us)
Async XLA Ops:
  0.0 0.7 copy-start
  2.2 2.0 %copy-start.2 = (bf16[512,1024]{1,0:T(8,128)(2,1)S(1)}, bf16[512,1024]{1,0:T(8,128)(2,1)}, u32[]{:S(2)}) copy-start(bf16[512,1024]{1,0:T(8,128)(2,1)} %param.8) | copy-start | bytes 3145732
  4.2 52.1 %copy-start.1 = (f32[2,192,512]{2,1,0:T(8,128)}, f32[2,192,512]{2,1,0:T(8,128)S(1)}, u32[]{:S(2)}) copy-start(f32[2,192,512]{2,1,0:T(8,128)S(1)} %pad_dynamic-update-slice_fusion.table_ref) | copy-start | bytes 2359300
